TPU v7x, 32 devices: a whole 2x2x4 slice. The times are simulated.
32 devices in a mesh: slab: 8 (over z, y), patch: 4 (over x, core).
Axes of the slice: x: 2, y: 2, z: 4, core: 2. Of those that a mesh axis runs over, the one named last changes fastest.
Arguments:
- fluid_state: float32 [16, 256, 256], P('slab', 'patch'), may hold values from -6 to 6
- fluid_rhs: float32 [16, 256, 256], P('slab', 'patch'), may hold values from -24 to 24
- element_scale: float32 [16, 256], P('slab', 'patch'), may hold values from 1 to 4
- element_matrix: bfloat16 [256, 256], replicated
- couple_x: bfloat16 [256, 256], replicated, may hold values from -0.09375 to 0.09375
- couple_y: bfloat16 [256, 256], replicated, may hold values from -0.09375 to 0.09375
- block_inverse: bfloat16 [256, 256], replicated
- traction_map: bfloat16 [3, 256], replicated, may hold values from -0.375 to 0.375
- slot_elem: int32 [8, 4, 1024], P('slab', 'patch'), may hold values from 0 to 127
- slot_point: int32 [8, 4, 1024], P('slab', 'patch'), may hold values from 0 to 8191
- slot_count: int32 [8, 4, 4], P('slab', 'patch'), may hold values from 0 to 256, as said below
- displacement: float32 [3, 256, 128], P(None, 'patch'), may hold values from -6 to 6
- stiffness: float32 [256, 128], P('patch'), may hold values from 0.03 to 0.3
Outputs:
- fluid_out: float32 [16, 256, 256], P('slab', 'patch')
- displacement_new: float32 [3, 256, 128], P(None, 'patch')
- wall_motion: float32 [3, 8, 4, 1024], P(None, 'slab', 'patch')
Inputs may be any that keep to these rules, and one draw needn't show every extreme that they name: For every block and owner only the first slot_count slots of that owner's 256 slots are live; the count 256 is reached for some block and owner in every draw.
All inputs are finite; a program needn't handle non-finite values.
Results may differ from a plain program's by a relative error of at most 0.0049.
Values may be sent and summed in bfloat16 or wider, within the bound.
A program may use at most 128 MiB of HBM per device.

v0:
```python
import functools

import jax
import jax.numpy as jnp
from jax import lax
from jax.experimental import pallas as pl
from jax.experimental.pallas import tpu as pltpu
from jax.sharding import PartitionSpec as P

SWEEPS = 3
PACK = 16
EDGE = 8
SPARE = 8 * 2**20
LOAD_ORDER = (0, 2, 3, 1, 8, 10, 9, 11, 12, 5, 4, 6, 7)
MESH = pl.DeviceIdType.MESH
F32 = jnp.float32
BF16 = jnp.bfloat16


def dot(a, b):
    return jnp.dot(a, b, preferred_element_type=F32)


def dot_nt(a, b):
    return lax.dot_general(a, b, (((1,), (1,)), ((), ())), preferred_element_type=F32)


def split_point(point, cols):
    if cols & (cols - 1) == 0:
        return lax.shift_right_logical(point, cols.bit_length() - 1), point & (cols - 1)
    row = lax.div(point, cols)
    return row, point - row * cols


def column(row_vector):
    n = row_vector.shape[1]
    shape = (n, n)
    eye = lax.broadcasted_iota(jnp.int32, shape, 0) == lax.broadcasted_iota(jnp.int32, shape, 1)
    return jnp.sum(jnp.where(eye, jnp.broadcast_to(row_vector, shape), 0.0), axis=1, keepdims=True)


def laplace(x):
    rows, cols = x.shape
    lane = lax.broadcasted_iota(jnp.int32, x.shape, 1)
    left = jnp.where(lane == 0, 0.0, pltpu.roll(x, 1, 1))
    right = jnp.where(lane == cols - 1, 0.0, pltpu.roll(x, cols - 1, 1))
    return 4.0 * x - (pltpu.roll(x, 1, 0) + pltpu.roll(x, rows - 1, 0) + left + right)


def kernel(slabs, patches, args, *refs):
    hbm, refs = refs[:args], refs[args:]
    (fluid_ref, net_ref, wall_ref), refs = refs[:3], refs[3:]
    staged, refs = refs[:args], refs[args:]
    (state_ref, rhs_ref, scale_ref, matrix_ref, cx_ref, cy_ref, inverse_ref, traction_ref) = staged[:8]
    (elem_ref, point_ref, count_ref, disp_ref, stiff_ref) = staged[8:]
    (vb, halo_x, halo_y, halo_d, points, pulls, pull_out, picks_out, picks_in) = refs[:9]
    (onehot_elem, onehot_row, onehot_col, rest_buf, gain_buf) = refs[9:14]
    (load_sem, sx, rx, sy, ry, sd, rd, sp1, rp1, sp2, rp2, sq1, rq1, sq2, rq2, sw, rw, near_sem) = refs[14:]

    loads_in = [pltpu.make_async_copy(hbm[n], staged[n], load_sem.at[n]) for n in range(args)]
    for n in LOAD_ORDER:
        loads_in[n].start()

    def ready(*names):
        for n in names:
            loads_in[n].wait()

    s = lax.axis_index("slab")
    p = lax.axis_index("patch")
    ex, ey, dof = state_ref.shape
    comps, rows, cols = disp_ref.shape
    cap = elem_ref.shape[2] // patches

    def slab_peer(j):
        return lax.rem(s + j, slabs)

    def patch_peer(j):
        return lax.rem(p + j, patches)

    def slab_sides(reach, semaphore):
        @pl.when(s >= reach)
        def _():
            pl.semaphore_signal(semaphore, inc=1, device_id=(s - reach, p), device_id_type=MESH)

        @pl.when(s + reach < slabs)
        def _():
            pl.semaphore_signal(semaphore, inc=1, device_id=(s + reach, p), device_id_type=MESH)

    def slab_count(reach):
        return jnp.where(s >= reach, 1, 0) + jnp.where(s + reach < slabs, 1, 0)

    reaches = []
    while 2 ** (len(reaches) + 1) < slabs - 1:
        reaches.append(2 ** (len(reaches) + 1))

    def near_signal(n):
        slab_sides(reaches[n], near_sem.at[n])

    def near_wait(n):
        pl.semaphore_wait(near_sem.at[n], slab_count(reaches[n]))

    barrier = pltpu.get_barrier_semaphore()
    for j in range(1, patches):
        pl.semaphore_signal(barrier, inc=1, device_id=(s, patch_peer(j)), device_id_type=MESH)
    slab_sides(1, barrier)
    awaited = patches - 1 + slab_count(1)

    def remote(src, dst, send, recv, target):
        return pltpu.make_async_remote_copy(
            src_ref=src, dst_ref=dst, send_sem=send, recv_sem=recv, device_id=target, device_id_type=MESH
        )

    def x_up(k):
        return remote(vb.at[k, ex - 1], halo_x.at[k, 0], sx.at[k, 0], rx.at[k, 0], (jnp.minimum(s + 1, slabs - 1), p))

    def x_down(k):
        return remote(vb.at[k, 0], halo_x.at[k, 1], sx.at[k, 1], rx.at[k, 1], (jnp.maximum(s - 1, 0), p))

    def y_up(k):
        return remote(
            vb.at[k, :, pl.ds(ey - PACK, PACK)], halo_y.at[k, 0], sy.at[k, 0], ry.at[k, 0],
            (s, jnp.minimum(p + 1, patches - 1)),
        )

    def y_down(k):
        return remote(
            vb.at[k, :, pl.ds(0, PACK)], halo_y.at[k, 1], sy.at[k, 1], ry.at[k, 1], (s, jnp.maximum(p - 1, 0))
        )

    def d_up():
        return remote(
            disp_ref.at[:, pl.ds(rows - EDGE, EDGE)], halo_d.at[0], sd.at[0], rd.at[0],
            (s, jnp.minimum(p + 1, patches - 1)),
        )

    def d_down():
        return remote(disp_ref.at[:, pl.ds(0, EDGE)], halo_d.at[1], sd.at[1], rd.at[1], (s, jnp.maximum(p - 1, 0)))

    has_prev_s, has_next_s = s > 0, s < slabs - 1
    has_prev_p, has_next_p = p > 0, p < patches - 1

    def point_first(j, mine):
        peer = patch_peer(j)
        src = point_ref.at[0, :, pl.ds(pl.multiple_of(peer * cap, cap), cap)]
        slot = p if mine else peer
        return remote(src, points.at[s, slot], sp1.at[j], rp1.at[slot], (s, peer))

    def point_second(j, mine):
        peer = slab_peer(j)
        slot = s if mine else peer
        return remote(points.at[s], points.at[slot], sp2.at[j], rp2.at[slot], (peer, p))

    def pull_first(j, mine):
        peer = patch_peer(j)
        slot = p if mine else peer
        return remote(pull_out.at[peer], pulls.at[s, slot], sq1.at[j], rq1.at[slot], (s, peer))

    def pull_second(j, mine):
        peer = slab_peer(j)
        slot = s if mine else peer
        return remote(pulls.at[s], pulls.at[slot], sq2.at[j], rq2.at[slot], (peer, p))

    def pick_copy(j, mine):
        peer = patch_peer(j)
        slot = p if mine else peer
        return remote(picks_out.at[peer], picks_in.at[slot], sw.at[j], rw.at[slot], (s, peer))

    def send_halos(k):
        pl.when(has_next_s)(lambda: x_up(k).start())
        pl.when(has_prev_s)(lambda: x_down(k).start())
        pl.when(has_next_p)(lambda: y_up(k).start())
        pl.when(has_prev_p)(lambda: y_down(k).start())

    ready(2)
    scales = [column(scale_ref[i : i + 1, :]) for i in range(ex)]
    inverses = [1.0 / x for x in scales]

    def build_points(slab):
        for k in range(patches):
            row, col = split_point(points[slab, k], cols)
            span = pl.ds(k * cap, cap)
            onehot_row[slab, :, span] = jnp.where(
                lax.broadcasted_iota(jnp.int32, (rows, cap), 0) == row, 1.0, 0.0
            ).astype(BF16)
            onehot_col[slab, :, span] = jnp.where(
                lax.broadcasted_iota(jnp.int32, (cols, cap), 0) == col, 1.0, 0.0
            ).astype(BF16)

    def lives(k):
        lane = lax.broadcasted_iota(jnp.int32, (1, cap), 1)
        return lane < count_ref[0, :, k : k + 1]

    def shell():
        pl.when(has_prev_p)(lambda: d_up().wait_recv())
        pl.when(has_next_p)(lambda: d_down().wait_recv())
        total = rows + 2 * EDGE
        line = lax.broadcasted_iota(jnp.int32, (total, cols), 0)
        first = jnp.where(has_prev_p, 0, EDGE)
        last = jnp.where(has_next_p, total, EDGE + rows)
        valid = (line >= first) & (line < last)
        gain = 1.0 / (36.0 * stiff_ref[...])
        gain_buf[...] = gain
        for c in range(comps):
            field = jnp.concatenate([halo_d[0, c], disp_ref[c], halo_d[1, c]], axis=0)
            field = jnp.where(valid, field, 0.0)
            bend = jnp.where(valid, laplace(field), 0.0)
            full = (laplace(bend) + 4.0 * bend)[EDGE : EDGE + rows]
            rest_buf[c] = disp_ref[c] - stiff_ref[...] * full * gain

    ready(0)
    v = state_ref[...]
    for k in range(SWEEPS):
        rounded = v.astype(BF16)
        vb[k] = rounded
        if k > 0:
            send_halos(k)
        if k == 0:
            ready(3, 1)
        own = dot(rounded.reshape(ex * ey, dof), matrix_ref[...]).reshape(ex, ey, dof)
        base = [rhs_ref[i] - scales[i] * own[i] for i in range(ex)]
        if k == 0:
            ready(8, 9, 10)
            for owner in range(patches):
                elem = elem_ref[0, :, owner * cap : (owner + 1) * cap]
                hit = (lax.broadcasted_iota(jnp.int32, (ex * ey, cap), 0) == elem) & lives(owner)
                onehot_elem[owner] = jnp.where(hit, 1.0, 0.0).astype(BF16)
            for owner in range(patches):

                @pl.when(p == owner)
                def _():
                    points[s, owner] = point_ref[0, :, owner * cap : (owner + 1) * cap]

            pl.semaphore_wait(barrier, awaited)
            send_halos(0)
            for j in range(1, patches):
                point_first(j, True).start()
            ready(11, 12)
            pl.when(has_next_p)(lambda: d_up().start())
            pl.when(has_prev_p)(lambda: d_down().start())
            ready(5, 4, 6, 7)
        if k == 1:
            if reaches:
                near_wait(0)
                if len(reaches) > 1:
                    near_signal(1)
            for j in range(1, patches):
                point_first(j, False).wait_recv()
            build_points(s)
        if k == 2:
            for n in range(1, len(reaches)):
                near_wait(n)
                if n + 1 < len(reaches):
                    near_signal(n + 1)
            for j in range(1, slabs):
                point_second(j, True).start()
            shell()

        wide = rounded.astype(F32)
        pl.when(has_prev_p)(lambda: y_up(k).wait_recv())
        pl.when(has_next_p)(lambda: y_down(k).wait_recv())
        line = lax.broadcasted_iota(jnp.int32, (ey, dof), 0)
        along_y = []
        for i in range(ex):
            before = halo_y[k, 0, i].astype(F32)[PACK - 1 : PACK]
            after = halo_y[k, 1, i].astype(F32)[0:1]
            before = jnp.where(has_prev_p, before, 0.0)
            after = jnp.where(has_next_p, after, 0.0)
            prev = jnp.where(line == 0, jnp.broadcast_to(before, (ey, dof)), pltpu.roll(wide[i], 1, 0))
            following = jnp.where(line == ey - 1, jnp.broadcast_to(after, (ey, dof)), pltpu.roll(wide[i], ey - 1, 0))
            along_y.append((prev + following).astype(BF16))
        side_y = dot(jnp.concatenate(along_y, axis=0), cy_ref[...])
        pl.when(has_prev_s)(lambda: x_up(k).wait_recv())
        pl.when(has_next_s)(lambda: x_down(k).wait_recv())
        if k == 0 and reaches:
            near_signal(0)
        low = jnp.where(has_prev_s, halo_x[k, 0].astype(F32), 0.0)
        high = jnp.where(has_next_s, halo_x[k, 1].astype(F32), 0.0)
        along_x = []
        for i in range(ex):
            below = low if i == 0 else wide[i - 1]
            above = high if i == ex - 1 else wide[i + 1]
            along_x.append((below + above).astype(BF16))
        side_x = dot(jnp.concatenate(along_x, axis=0), cx_ref[...])
        side = (side_x + side_y).reshape(ex, ey, dof)
        residue = jnp.concatenate([(base[i] + side[i]).astype(BF16) for i in range(ex)], axis=0)
        update = dot(residue, inverse_ref[...]).reshape(ex, ey, dof)
        v = jnp.stack([v[i] + update[i] * inverses[i] for i in range(ex)], axis=0)

    final = v.astype(BF16).reshape(ex * ey, dof)
    traction = dot_nt(traction_ref[...], final).astype(BF16)
    for owner in range(patches):
        pull_out[owner] = dot(traction, onehot_elem[owner]).astype(BF16)
    for j in range(1, patches):
        pull_first(j, True).start()
    pulls[s, p] = pull_out[p]
    fluid_ref[...] = v
    for j in range(1, patches):
        pull_first(j, False).wait_recv()
    for j in range(1, slabs):
        pull_second(j, True).start()

    def scatter(slab, acc):
        for k in range(patches):
            span = pl.ds(k * cap, cap)
            hot = onehot_row[slab, :, span]
            value = pulls[slab, k]
            scaled = jnp.concatenate([hot * value[c : c + 1] for c in range(comps)], axis=0)
            acc = acc + dot_nt(scaled, onehot_col[slab, :, span])
        return acc

    def arrive(j, carry):
        point_second(j, False).wait_recv()
        build_points(slab_peer(j))
        return carry

    lax.fori_loop(1, slabs, arrive, 0)
    acc = scatter(s, jnp.zeros((comps * rows, cols), F32))

    def gathered(j, acc):
        pull_second(j, False).wait_recv()
        return scatter(slab_peer(j), acc)

    acc = lax.fori_loop(1, slabs, gathered, acc)
    loads = acc.reshape(comps, rows, cols)
    fresh = [rest_buf[c] + loads[c] * gain_buf[...] for c in range(comps)]
    narrow = jnp.concatenate([x.astype(BF16) for x in fresh], axis=0)
    for k in range(patches):
        span = pl.ds(k * cap, cap)
        spread = dot(narrow, onehot_col[s, :, span]).reshape(comps, rows, cap)
        hot = onehot_row[s, :, span].astype(F32)
        for c in range(comps):
            picks_out[k, c : c + 1] = jnp.sum(spread[c] * hot, axis=0, keepdims=True)
    for j in range(1, patches):
        pick_copy(j, True).start()
    picks_in[p] = picks_out[p]
    for c in range(comps):
        net_ref[c] = fresh[c]
    for j in range(1, patches):
        pick_copy(j, False).wait_recv()
    for k in range(patches):
        live = lives(k)
        for c in range(comps):
            wall_ref[c, 0, :, k * cap : (k + 1) * cap] = jnp.where(live, picks_in[k, c : c + 1], 0.0)

    for k in range(SWEEPS):
        pl.when(has_next_s)(lambda: x_up(k).wait_send())
        pl.when(has_prev_s)(lambda: x_down(k).wait_send())
        pl.when(has_next_p)(lambda: y_up(k).wait_send())
        pl.when(has_prev_p)(lambda: y_down(k).wait_send())
    pl.when(has_next_p)(lambda: d_up().wait_send())
    pl.when(has_prev_p)(lambda: d_down().wait_send())
    for j in range(1, patches):
        point_first(j, True).wait_send()
        pull_first(j, True).wait_send()
        pick_copy(j, True).wait_send()
    for j in range(1, slabs):
        point_second(j, True).wait_send()
        pull_second(j, True).wait_send()


def deliver(*refs):
    copies = [pltpu.make_async_copy(refs[n], refs[n + 3], refs[6].at[n]) for n in range(3)]
    for copy in copies:
        copy.start()
    for copy in copies:
        copy.wait()


def shards(slabs, patches, *args):
    state, disp, elem = args[0], args[11], args[8]
    ex, ey, dof = state.shape
    comps, rows, cols = disp.shape
    cap = elem.shape[2] // patches
    sem = pltpu.SemaphoreType.DMA
    vmem = pl.BlockSpec(memory_space=pltpu.VMEM)
    hot_bytes = slabs * patches * cap * (rows + cols) * 2
    outs = pl.pallas_call(
        functools.partial(kernel, slabs, patches, len(args)),
        out_shape=(
            jax.ShapeDtypeStruct(state.shape, F32),
            jax.ShapeDtypeStruct(disp.shape, F32),
            jax.ShapeDtypeStruct((comps, 1, 1, elem.shape[2]), F32),
        ),
        in_specs=[pl.BlockSpec(memory_space=pltpu.HBM)] * len(args),
        out_specs=(vmem, vmem, vmem),
        scratch_shapes=[pltpu.VMEM(x.shape, x.dtype) for x in args]
        + [
            pltpu.VMEM((SWEEPS, ex, ey, dof), BF16),
            pltpu.VMEM((SWEEPS, 2, ey, dof), BF16),
            pltpu.VMEM((SWEEPS, 2, ex, PACK, dof), BF16),
            pltpu.VMEM((2, comps, EDGE, cols), F32),
            pltpu.VMEM((slabs, patches, 1, cap), jnp.int32),
            pltpu.VMEM((slabs, patches, comps, cap), BF16),
            pltpu.VMEM((patches, comps, cap), BF16),
            pltpu.VMEM((patches, comps, cap), F32),
            pltpu.VMEM((patches, comps, cap), F32),
            pltpu.VMEM((patches, ex * ey, cap), BF16),
            pltpu.VMEM((slabs, rows, patches * cap), BF16),
            pltpu.VMEM((slabs, cols, patches * cap), BF16),
            pltpu.VMEM((comps, rows, cols), F32),
            pltpu.VMEM((rows, cols), F32),
            sem((len(args),)),
            sem((SWEEPS, 2)),
            sem((SWEEPS, 2)),
            sem((SWEEPS, 2)),
            sem((SWEEPS, 2)),
            sem((2,)),
            sem((2,)),
            sem((patches,)),
            sem((patches,)),
            sem((slabs,)),
            sem((slabs,)),
            sem((patches,)),
            sem((patches,)),
            sem((slabs,)),
            sem((slabs,)),
            sem((patches,)),
            sem((patches,)),
            pltpu.SemaphoreType.REGULAR((max(slabs.bit_length(), 1),)),
        ],
        compiler_params=pltpu.CompilerParams(collective_id=0, has_side_effects=True),
    )(*args)
    return pl.pallas_call(
        deliver,
        out_shape=tuple(jax.ShapeDtypeStruct(x.shape, x.dtype) for x in outs),
        in_specs=[vmem] * 3,
        out_specs=(pl.BlockSpec(memory_space=pltpu.HBM),) * 3,
        scratch_shapes=[sem((3,))],
    )(*outs)


def solution(mesh):
    return jax.shard_map(
        functools.partial(shards, mesh.shape["slab"], mesh.shape["patch"]),
        mesh=mesh,
        in_specs=(
            P("slab", "patch", None),
            P("slab", "patch", None),
            P("slab", "patch"),
            P(),
            P(),
            P(),
            P(),
            P(),
            P("slab", "patch", None),
            P("slab", "patch", None),
            P("slab", "patch", None),
            P(None, "patch", None),
            P("patch", None),
        ),
        out_specs=(
            P("slab", "patch", None),
            P(None, "patch", None),
            P(None, "slab", "patch", None),
        ),
        check_vma=False,
    )
```

profile of v0, /device:TPU:0, one launch (start us, length us, event | category | flops | bytes accessed | tf_op | source)
XLA Modules:
  0.0 30.2 jit_solution(5291540954155538353)
XLA Ops:
  0.6 27.9 %shard_map.148 = (f32[2,64,256]{2,1,0:T(8,128)}, f32[3,64,128]{2,1,0:T(8,128)}, f32[3,1,1,1024]{3,2,1,0:T(1,128)}) custom-call(f32[2,64,256]{2,1,0:T(8,128)} %refs_0_.1, f32[2,64,256]{2,1,0:T(8,128)} %refs_1_.1, f32[2,64]{1,0:T(2,128)} %refs_2_.1, bf16[256,256]{1,0:T(8,128)(2,1)} %refs_3_.1, bf16[256,256]{1,0:T(8,128)(2,1)} %refs_4_.1, ...), custom_call_target="tpu_custom_call" | custom-call | tf_op jit(solution)/shard_map/pallas_call | solution.py:377
  28.6 1.7 %shard_map.149 = (f32[2,64,256]{2,1,0:T(8,128)}, f32[3,64,128]{2,1,0:T(8,128)}, f32[3,1,1,1024]{3,2,1,0:T(1,128)}) custom-call(f32[2,64,256]{2,1,0:T(8,128)} %get-tuple-element.6.refs_0_, f32[3,64,128]{2,1,0:T(8,128)} %get-tuple-element.7.refs_1_, f32[3,1,1,1024]{3,2,1,0:T(1,128)} %get-tuple-element.8.refs_2_), custom_call_target="tpu_custom_call" | custom-call | tf_op jit(solution)/shard_map/pallas_call | solution.py:423
where the time goes:
time: 30.4 us; the launch traced here: 30.2 us
  Pallas kernels  29.6 us (97%)
  between operations  0.64 us (2%)
    pallas_call x1, Pallas kernels, shards(): pl.pallas_call(functools.partial(kernel, slabs, patches, len(args)), out_...  27.9 us
    pallas_call x1, Pallas kernels, shards(): pl.pallas_call(deliver, out_shape=tuple((jax.ShapeDtypeStruct(x.shape, x....  1.66 us

commit v1 on v0

--- a/solution.py
+++ b/solution.py
@@ -11,7 +11,8 @@
 PACK = 16
 EDGE = 8
 SPARE = 8 * 2**20
-LOAD_ORDER = (0, 2, 3, 1, 8, 10, 9, 11, 12, 5, 4, 6, 7)
+DEEP = 16
+LOAD_ORDER = (7, 6, 3, 4, 5, 2, 0, 1, 9, 8, 10, 11, 12)
 MESH = pl.DeviceIdType.MESH
 F32 = jnp.float32
 BF16 = jnp.bfloat16
@@ -45,6 +46,34 @@
     left = jnp.where(lane == 0, 0.0, pltpu.roll(x, 1, 1))
     right = jnp.where(lane == cols - 1, 0.0, pltpu.roll(x, cols - 1, 1))
     return 4.0 * x - (pltpu.roll(x, 1, 0) + pltpu.roll(x, rows - 1, 0) + left + right)
+
+
+def join(*parts):
+    return jnp.concatenate(parts, axis=0)
+
+
+def blank(rows, cols):
+    return jnp.zeros((rows, cols), F32)
+
+
+def make_words(traction, inverse, matrix, couple_x, couple_y):
+    comps, dof = traction.shape
+    base0 = dot_nt(traction, inverse)
+    low = base0.astype(BF16)
+    one = join(dot_nt(low, couple_x), traction.astype(F32) - dot_nt(low, matrix), dot_nt(low, couple_y))
+    base1 = dot_nt(one.astype(BF16), inverse)
+    low = base1.astype(BF16)
+    by_x, by_y = dot_nt(low, couple_x), dot_nt(low, couple_y)
+    by_d = one - dot_nt(low, matrix)
+    two = join(
+        by_d[:comps], by_x, by_y[:comps], blank(DEEP - 5 * comps, dof),
+        by_d[comps:], by_y[comps:], blank(DEEP - 4 * comps, dof),
+    )
+    base2 = dot_nt(two.astype(BF16), inverse)
+    low = base2.astype(BF16)
+    three = join(two - dot_nt(low, matrix), dot_nt(low, couple_x), dot_nt(low, couple_y))
+    rest = join(base2, base1, blank(DEEP - 3 * comps, dof), base0, blank(DEEP - comps, dof))
+    return three.astype(BF16), rest.astype(BF16)
 
 
 def kernel(slabs, patches, args, *refs):
@@ -55,7 +84,9 @@
     (elem_ref, point_ref, count_ref, disp_ref, stiff_ref) = staged[8:]
     (vb, halo_x, halo_y, halo_d, points, pulls, pull_out, picks_out, picks_in) = refs[:9]
     (onehot_elem, onehot_row, onehot_col, rest_buf, gain_buf) = refs[9:14]
-    (load_sem, sx, rx, sy, ry, sd, rd, sp1, rp1, sp2, rp2, sq1, rq1, sq2, rq2, sw, rw, near_sem) = refs[14:]
+    (near_out, near_in, far_out, far_in, side_out, side_in, tip_out, tip_in, w_out, w_in) = refs[14:24]
+    (load_sem, sx, rx, sy, ry, sd, rd, sp1, rp1, sp2, rp2, sq, rq, sw, rw) = refs[24:39]
+    (s_near, r_near, s_far, r_far, s_side, r_side, s_tip, r_tip, s_w, r_w, near_sem) = refs[39:]
 
     loads_in = [pltpu.make_async_copy(hbm[n], staged[n], load_sem.at[n]) for n in range(args)]
     for n in LOAD_ORDER:
@@ -70,6 +101,7 @@
     ex, ey, dof = state_ref.shape
     comps, rows, cols = disp_ref.shape
     cap = elem_ref.shape[2] // patches
+    wide_lanes = ex * ey
 
     def slab_peer(j):
         return lax.rem(s + j, slabs)
@@ -99,45 +131,87 @@
     def near_wait(n):
         pl.semaphore_wait(near_sem.at[n], slab_count(reaches[n]))
 
+    has_prev_s, has_next_s = s > 0, s < slabs - 1
+    has_prev_p, has_next_p = p > 0, p < patches - 1
+    has_far_prev, has_far_next = s > 1, s < slabs - 2
+
     barrier = pltpu.get_barrier_semaphore()
     for j in range(1, patches):
         pl.semaphore_signal(barrier, inc=1, device_id=(s, patch_peer(j)), device_id_type=MESH)
-    slab_sides(1, barrier)
-    awaited = patches - 1 + slab_count(1)
+    for reach in (1, 2):
+
+        @pl.when(s >= reach)
+        def _():
+            for j in range(patches):
+                pl.semaphore_signal(barrier, inc=1, device_id=(s - reach, patch_peer(j)), device_id_type=MESH)
+
+        @pl.when(s + reach < slabs)
+        def _():
+            for j in range(patches):
+                pl.semaphore_signal(barrier, inc=1, device_id=(s + reach, patch_peer(j)), device_id_type=MESH)
+
+    awaited = patches - 1 + patches * (slab_count(1) + slab_count(2))
 
     def remote(src, dst, send, recv, target):
         return pltpu.make_async_remote_copy(
             src_ref=src, dst_ref=dst, send_sem=send, recv_sem=recv, device_id=target, device_id_type=MESH
         )
 
+    def slab_at(step):
+        return jnp.clip(s + step, 0, slabs - 1)
+
+    def patch_at(step):
+        return jnp.clip(p + step, 0, patches - 1)
+
     def x_up(k):
-        return remote(vb.at[k, ex - 1], halo_x.at[k, 0], sx.at[k, 0], rx.at[k, 0], (jnp.minimum(s + 1, slabs - 1), p))
+        return remote(vb.at[k, ex - 1], halo_x.at[k, 0], sx.at[k, 0], rx.at[k, 0], (slab_at(1), p))
 
     def x_down(k):
-        return remote(vb.at[k, 0], halo_x.at[k, 1], sx.at[k, 1], rx.at[k, 1], (jnp.maximum(s - 1, 0), p))
+        return remote(vb.at[k, 0], halo_x.at[k, 1], sx.at[k, 1], rx.at[k, 1], (slab_at(-1), p))
 
     def y_up(k):
         return remote(
-            vb.at[k, :, pl.ds(ey - PACK, PACK)], halo_y.at[k, 0], sy.at[k, 0], ry.at[k, 0],
-            (s, jnp.minimum(p + 1, patches - 1)),
+            vb.at[k, :, pl.ds(ey - PACK, PACK)], halo_y.at[k, 0], sy.at[k, 0], ry.at[k, 0], (s, patch_at(1))
         )
 
     def y_down(k):
-        return remote(
-            vb.at[k, :, pl.ds(0, PACK)], halo_y.at[k, 1], sy.at[k, 1], ry.at[k, 1], (s, jnp.maximum(p - 1, 0))
-        )
+        return remote(vb.at[k, :, pl.ds(0, PACK)], halo_y.at[k, 1], sy.at[k, 1], ry.at[k, 1], (s, patch_at(-1)))
 
     def d_up():
-        return remote(
-            disp_ref.at[:, pl.ds(rows - EDGE, EDGE)], halo_d.at[0], sd.at[0], rd.at[0],
-            (s, jnp.minimum(p + 1, patches - 1)),
-        )
+        return remote(disp_ref.at[:, pl.ds(rows - EDGE, EDGE)], halo_d.at[0], sd.at[0], rd.at[0], (s, patch_at(1)))
 
     def d_down():
-        return remote(disp_ref.at[:, pl.ds(0, EDGE)], halo_d.at[1], sd.at[1], rd.at[1], (s, jnp.maximum(p - 1, 0)))
-
-    has_prev_s, has_next_s = s > 0, s < slabs - 1
-    has_prev_p, has_next_p = p > 0, p < patches - 1
+        return remote(disp_ref.at[:, pl.ds(0, EDGE)], halo_d.at[1], sd.at[1], rd.at[1], (s, patch_at(-1)))
+
+    def near_copy(n):
+        return remote(near_out, near_in.at[n], s_near.at[n], r_near.at[n], (slab_at(1 - 2 * n), p))
+
+    def far_copy(n):
+        return remote(far_out, far_in.at[n], s_far.at[n], r_far.at[n], (slab_at(2 - 4 * n), p))
+
+    def side_copy(n):
+        return remote(side_out.at[n], side_in.at[n], s_side.at[n], r_side.at[n], (s, patch_at(1 - 2 * n)))
+
+    def tip_copy(n, m):
+        q = 2 * n + m
+        return remote(tip_out.at[q], tip_in.at[q], s_tip.at[q], r_tip.at[q], (slab_at(1 - 2 * n), patch_at(1 - 2 * m)))
+
+    def w_copy(a, b):
+        q = 3 * (1 - a) + 1 - b
+        return remote(w_out, w_in.at[q], s_w.at[q], r_w.at[q], (slab_at(a), patch_at(b)))
+
+    to_s, from_s = (has_next_s, has_prev_s), (has_prev_s, has_next_s)
+    to_p, from_p = (has_next_p, has_prev_p), (has_prev_p, has_next_p)
+    to_far, from_far = (has_far_next, has_far_prev), (has_far_prev, has_far_next)
+    corners = [(n, m) for n in range(2) for m in range(2)]
+    around = [(a, b) for a in (-1, 0, 1) for b in (-1, 0, 1) if (a, b) != (0, 0)]
+
+    def exists(a, b):
+        ok_s = {-1: has_prev_s, 0: None, 1: has_next_s}[a]
+        ok_p = {-1: has_prev_p, 0: None, 1: has_next_p}[b]
+        if ok_s is None:
+            return ok_p
+        return ok_s if ok_p is None else jnp.logical_and(ok_s, ok_p)
 
     def point_first(j, mine):
         peer = patch_peer(j)
@@ -150,15 +224,12 @@
         slot = s if mine else peer
         return remote(points.at[s], points.at[slot], sp2.at[j], rp2.at[slot], (peer, p))
 
-    def pull_first(j, mine):
-        peer = patch_peer(j)
-        slot = p if mine else peer
-        return remote(pull_out.at[peer], pulls.at[s, slot], sq1.at[j], rq1.at[slot], (s, peer))
-
-    def pull_second(j, mine):
-        peer = slab_peer(j)
-        slot = s if mine else peer
-        return remote(pulls.at[s], pulls.at[slot], sq2.at[j], rq2.at[slot], (peer, p))
+    def pull_copy(j, i):
+        to = (slab_peer(j), patch_peer(i))
+        return remote(pull_out.at[to[1]], pulls.at[s, p], sq.at[j, i], rq.at[s, p], to)
+
+    def pull_arrival(slab, patch):
+        return remote(pull_out.at[p], pulls.at[slab, patch], sq.at[0, 0], rq.at[slab, patch], (slab, patch))
 
     def pick_copy(j, mine):
         peer = patch_peer(j)
@@ -170,10 +241,6 @@
         pl.when(has_prev_s)(lambda: x_down(k).start())
         pl.when(has_next_p)(lambda: y_up(k).start())
         pl.when(has_prev_p)(lambda: y_down(k).start())
-
-    ready(2)
-    scales = [column(scale_ref[i : i + 1, :]) for i in range(ex)]
-    inverses = [1.0 / x for x in scales]
 
     def build_points(slab):
         for k in range(patches):
@@ -207,57 +274,238 @@
             full = (laplace(bend) + 4.0 * bend)[EDGE : EDGE + rows]
             rest_buf[c] = disp_ref[c] - stiff_ref[...] * full * gain
 
+    with jax.named_scope("words"):
+        ready(7, 6, 4, 3, 5)
+        words, rest = make_words(
+            traction_ref[...], inverse_ref[...], matrix_ref[...], cx_ref[...], cy_ref[...]
+        )
+    ready(2)
+    w_out[...] = blank(*w_out.shape)
+    w_out[:, 0:ey] = 1.0 / scale_ref[...]
     ready(0)
-    v = state_ref[...]
-    for k in range(SWEEPS):
-        rounded = v.astype(BF16)
-        vb[k] = rounded
-        if k > 0:
-            send_halos(k)
-        if k == 0:
-            ready(3, 1)
+    rounded0 = state_ref[...].astype(BF16)
+    vb[0] = rounded0
+    ready(1)
+    wet = rhs_ref[...].astype(BF16)
+    with jax.named_scope("project"):
+        own_v = dot_nt(words, rounded0.reshape(wide_lanes, dof))
+        own_r = dot_nt(rest, wet.reshape(wide_lanes, dof))
+        spare = join(blank(2 * DEEP - comps - 1, wide_lanes), own_r[2 * DEEP : 2 * DEEP + comps], blank(1, wide_lanes))
+        near_out[...] = join(
+            own_v[0:DEEP], own_v[2 * DEEP : 4 * DEEP] + spare, own_v[4 * DEEP : 5 * DEEP], own_r[0:DEEP]
+        ).astype(BF16)
+        far_out[...] = own_v[2 * DEEP : 2 * DEEP + 8].astype(BF16)
+
+        def state_at(i, c):
+            return state_ref[i, c : c + 1]
+
+        def rhs_at(i, c):
+            return rhs_ref[i, c : c + 1]
+
+        for m in range(2):
+            edge = [ey - 1 - j if m == 0 else j for j in range(SWEEPS)]
+            lines = [state_at(i, c) for i in range(ex) for c in edge]
+            lines += [rhs_at(i, c) for i in range(ex) for c in edge[: SWEEPS - 1]]
+            side_out[m] = join(*lines, blank(DEEP - len(lines), dof)).astype(BF16)
+            for n in range(2):
+                order = [ex - 1, ex - 2] if n == 0 else [0, 1]
+                tip_out[2 * n + m] = join(
+                    state_at(order[0], edge[0]),
+                    state_at(order[0], edge[1]),
+                    state_at(order[1], edge[0]),
+                    rhs_at(order[0], edge[0]),
+                ).astype(BF16)
+
+    with jax.named_scope("w_barrier"):
+        pl.semaphore_wait(barrier, awaited)
+    for n in range(2):
+        pl.when(to_s[n])(lambda: near_copy(n).start())
+    for n, m in corners:
+        pl.when(jnp.logical_and(to_s[n], to_p[m]))(lambda: tip_copy(n, m).start())
+    for n in range(2):
+        pl.when(to_far[n])(lambda: far_copy(n).start())
+    for m in range(2):
+        pl.when(to_p[m])(lambda: side_copy(m).start())
+    for a, b in around:
+        pl.when(exists(a, b))(lambda: w_copy(a, b).start())
+    if reaches:
+        near_signal(0)
+    ready(9)
+    for j in range(1, patches):
+        point_first(j, True).start()
+    ready(11)
+    pl.when(has_next_p)(lambda: d_up().start())
+    pl.when(has_prev_p)(lambda: d_down().start())
+    ready(8, 10, 12)
+    for owner in range(patches):
+
+        @pl.when(p == owner)
+        def _():
+            points[s, owner] = point_ref[0, :, owner * cap : (owner + 1) * cap]
+
+    for owner in range(patches):
+        elem = elem_ref[0, :, owner * cap : (owner + 1) * cap]
+        hit = (lax.broadcasted_iota(jnp.int32, (wide_lanes, cap), 0) == elem) & lives(owner)
+        onehot_elem[owner] = jnp.where(hit, 1.0, 0.0).astype(BF16)
+    for n in range(len(reaches)):
+        with jax.named_scope("w_reach"):
+            near_wait(n)
+        if n + 1 < len(reaches):
+            near_signal(n + 1)
+        if n == 0:
+            send_halos(0)
+            with jax.named_scope("w_pt1"):
+                for j in range(1, patches):
+                    point_first(j, False).wait_recv()
+            build_points(s)
+    if not reaches:
+        send_halos(0)
+        for j in range(1, patches):
+            point_first(j, False).wait_recv()
+        build_points(s)
+    for j in range(1, slabs):
+        point_second(j, True).start()
+    with jax.named_scope("shell"):
+        shell()
+    scales = [column(scale_ref[i : i + 1, :]) for i in range(ex)]
+    inverses = [1.0 / x for x in scales]
+
+    lane = lax.broadcasted_iota(jnp.int32, (1, wide_lanes), 1)
+    low_half = lane < ey
+    tail_half = lane < ey + ey // 2
+
+    def halves(x):
+        return jnp.where(low_half, x, 0.0), jnp.where(low_half, pltpu.roll(x, ey, 1), 0.0)
+
+    span_rows = list(range(-ex, 2 * ex))
+    spots_v, spots_r = [], []
+    for m in range(2):
+        def spot(r, j):
+            return (r + ex) * wide_lanes + (wide_lanes - j if m == 0 else ey + j - 1)
+
+        for i in range(ex):
+            spots_v += [(m * DEEP + i * SWEEPS + j - 1, spot(i, j)) for j in range(1, SWEEPS + 1)]
+            first = m * DEEP + ex * SWEEPS + i * (SWEEPS - 1) - 1
+            spots_r += [(first + j, spot(i, j)) for j in range(1, SWEEPS)]
+        for n in range(2):
+            r1, r2 = (-1, -2) if n == 0 else (ex, ex + 1)
+            first = 2 * DEEP + 4 * (2 * n + m)
+            spots_v += [(first, spot(r1, 1)), (first + 1, spot(r1, 2)), (first + 2, spot(r2, 1))]
+            spots_r += [(first + 3, spot(r1, 1))]
+
+    def placing(spots):
+        line = lax.broadcasted_iota(jnp.int32, (3 * DEEP, 1), 0)
+        target = jnp.full((3 * DEEP, 1), -1, jnp.int32)
+        for n, at in spots:
+            target = jnp.where(line == n, at, target)
+        lanes = lax.broadcasted_iota(jnp.int32, (3 * DEEP, len(span_rows) * wide_lanes), 1)
+        return jnp.where(lanes == target, 1.0, 0.0).astype(BF16)
+
+    with jax.named_scope("w_side"):
+        for m in range(2):
+            pl.when(from_p[m])(lambda: side_copy(m).wait_recv())
+        for a, b in around:
+            pl.when(exists(-a, -b))(lambda: w_copy(a, b).wait_recv())
+        for n, m in corners:
+            pl.when(jnp.logical_and(from_s[n], from_p[m]))(lambda: tip_copy(n, m).wait_recv())
+    with jax.named_scope("place"):
+        stack = join(
+            *[jnp.where(from_p[m], side_in[m].astype(F32), 0.0) for m in range(2)],
+            *[
+                jnp.where(jnp.logical_and(from_s[n], from_p[m]), tip_in[2 * n + m].astype(F32), 0.0)
+                for n, m in corners
+            ],
+        ).astype(BF16)
+        placed_v = dot(dot_nt(words, stack).astype(BF16), placing(spots_v))
+        placed_r = dot(dot_nt(rest, stack).astype(BF16), placing(spots_r))
+
+        def piece(x, r):
+            return x[:, (r + ex) * wide_lanes : (r + ex + 1) * wide_lanes]
+
+        def weight(a, b):
+            if (a, b) == (0, 0):
+                return w_out[...]
+            return jnp.where(exists(a, b), w_in[3 * (a + 1) + b + 1], 0.0)
+
+        w_rows = {}
+        for a in (-1, 0, 1):
+            middle = weight(a, 0)
+            before, after = pltpu.roll(weight(a, -1), ey, 1), pltpu.roll(weight(a, 1), ey, 1)
+            both = jnp.where(low_half, middle, jnp.where(tail_half, after, before))
+            for i in range(ex):
+                w_rows[a * ex + i] = both[i : i + 1]
+
+    with jax.named_scope("w_near"):
+        for n in range(2):
+            pl.when(from_far[n])(lambda: far_copy(n).wait_recv())
+            pl.when(from_s[n])(lambda: near_copy(n).wait_recv())
+
+    with jax.named_scope("stencil"):
+        by_d, by_x, by_y, by_r2, by_r1, by_r0 = {}, {}, {}, {}, {}, {}
+        for i, (v_half, r_half) in enumerate(zip(halves(own_v), halves(own_r))):
+            full, side = v_half + piece(placed_v, i), r_half + piece(placed_r, i)
+            by_d[i], by_x[i], by_y[i] = (full[k * 2 * DEEP : (k + 1) * 2 * DEEP] for k in range(3))
+            by_r2[i], by_r1[i], by_r0[i] = (
+                side[: 2 * DEEP], side[2 * DEEP : 2 * DEEP + 3 * comps], side[3 * DEEP : 3 * DEEP + comps]
+            )
+        for n in range(2):
+            got = jnp.where(from_s[n], near_in[n].astype(F32), 0.0)
+            for i, half in enumerate(halves(got)):
+                r = i - ex if n == 0 else i + ex
+                edge_v, edge_r = piece(placed_v, r), piece(placed_r, r)
+                by_d[r] = half[0:DEEP] + edge_v[0:DEEP]
+                by_x[r] = half[DEEP : 3 * DEEP] + edge_v[2 * DEEP : 4 * DEEP]
+                by_y[r] = half[3 * DEEP : 4 * DEEP] + edge_v[4 * DEEP : 5 * DEEP]
+                by_r2[r] = half[4 * DEEP : 5 * DEEP] + edge_r[0:DEEP]
+                by_r1[r] = half[3 * DEEP - comps - 1 : 3 * DEEP - 1]
+            beyond = halves(jnp.where(from_far[n], far_in[n].astype(F32), 0.0))[1 - n]
+            by_x[-ex - 1 if n == 0 else 2 * ex] = join(beyond, blank(DEEP - 8, wide_lanes))
+
+        def turn(x):
+            return pltpu.roll(x, 1, 1) + pltpu.roll(x, wide_lanes - 1, 1)
+
+        one = {}
+        for r in span_rows:
+            n = 2 * DEEP if 0 <= r < ex else DEEP
+            one[r] = by_d[r] + w_rows[r] * (by_x[r - 1][:n] + by_x[r + 1][:n] + turn(by_y[r]) + by_r2[r])
+        two = {}
+        for r in range(-1, ex + 1):
+            if 0 <= r < ex:
+                d_part = join(one[r][:comps], one[r][DEEP : DEEP + 2 * comps])
+                y_part = join(one[r][4 * comps : 5 * comps], one[r][DEEP + 2 * comps : DEEP + 4 * comps])
+                n = 3 * comps
+            else:
+                d_part, y_part = one[r][:comps], one[r][4 * comps : 5 * comps]
+                n = comps
+            x_part = one[r - 1][comps : comps + n] + one[r + 1][comps : comps + n]
+            two[r] = d_part + w_rows[r] * (x_part + turn(y_part) + by_r1[r])
+        drawn = []
+        for r in range(ex):
+            x_part = two[r - 1][:comps] + two[r + 1][:comps]
+            drawn.append(
+                two[r][comps : 2 * comps]
+                + w_rows[r] * (x_part + turn(two[r][2 * comps : 3 * comps]) + by_r0[r])
+            )
+        traction = jnp.where(low_half, drawn[0], pltpu.roll(drawn[1], ey, 1)).astype(BF16)
+        for owner in range(patches):
+            pull_out[owner] = dot(traction, onehot_elem[owner]).astype(BF16)
+    with jax.named_scope("s_pull"):
+        for j in sorted(range(slabs), key=lambda j: -min(j, slabs - j)):
+            for i in range(patches):
+                if (j, i) != (0, 0):
+                    pull_copy(j, i).start()
+    pulls[s, p] = pull_out[p]
+
+    def sweep(k, v):
+        rounded = rounded0 if k == 0 else vb[k]
         own = dot(rounded.reshape(ex * ey, dof), matrix_ref[...]).reshape(ex, ey, dof)
         base = [rhs_ref[i] - scales[i] * own[i] for i in range(ex)]
-        if k == 0:
-            ready(8, 9, 10)
-            for owner in range(patches):
-                elem = elem_ref[0, :, owner * cap : (owner + 1) * cap]
-                hit = (lax.broadcasted_iota(jnp.int32, (ex * ey, cap), 0) == elem) & lives(owner)
-                onehot_elem[owner] = jnp.where(hit, 1.0, 0.0).astype(BF16)
-            for owner in range(patches):
-
-                @pl.when(p == owner)
-                def _():
-                    points[s, owner] = point_ref[0, :, owner * cap : (owner + 1) * cap]
-
-            pl.semaphore_wait(barrier, awaited)
-            send_halos(0)
-            for j in range(1, patches):
-                point_first(j, True).start()
-            ready(11, 12)
-            pl.when(has_next_p)(lambda: d_up().start())
-            pl.when(has_prev_p)(lambda: d_down().start())
-            ready(5, 4, 6, 7)
-        if k == 1:
-            if reaches:
-                near_wait(0)
-                if len(reaches) > 1:
-                    near_signal(1)
-            for j in range(1, patches):
-                point_first(j, False).wait_recv()
-            build_points(s)
-        if k == 2:
-            for n in range(1, len(reaches)):
-                near_wait(n)
-                if n + 1 < len(reaches):
-                    near_signal(n + 1)
-            for j in range(1, slabs):
-                point_second(j, True).start()
-            shell()
-
         wide = rounded.astype(F32)
-        pl.when(has_prev_p)(lambda: y_up(k).wait_recv())
-        pl.when(has_next_p)(lambda: y_down(k).wait_recv())
+        with jax.named_scope("w_halo"):
+            pl.when(has_prev_p)(lambda: y_up(k).wait_recv())
+            pl.when(has_next_p)(lambda: y_down(k).wait_recv())
+            pl.when(has_prev_s)(lambda: x_up(k).wait_recv())
+            pl.when(has_next_s)(lambda: x_down(k).wait_recv())
         line = lax.broadcasted_iota(jnp.int32, (ey, dof), 0)
         along_y = []
         for i in range(ex):
@@ -269,10 +517,6 @@
             following = jnp.where(line == ey - 1, jnp.broadcast_to(after, (ey, dof)), pltpu.roll(wide[i], ey - 1, 0))
             along_y.append((prev + following).astype(BF16))
         side_y = dot(jnp.concatenate(along_y, axis=0), cy_ref[...])
-        pl.when(has_prev_s)(lambda: x_up(k).wait_recv())
-        pl.when(has_next_s)(lambda: x_down(k).wait_recv())
-        if k == 0 and reaches:
-            near_signal(0)
         low = jnp.where(has_prev_s, halo_x[k, 0].astype(F32), 0.0)
         high = jnp.where(has_next_s, halo_x[k, 1].astype(F32), 0.0)
         along_x = []
@@ -284,20 +528,17 @@
         side = (side_x + side_y).reshape(ex, ey, dof)
         residue = jnp.concatenate([(base[i] + side[i]).astype(BF16) for i in range(ex)], axis=0)
         update = dot(residue, inverse_ref[...]).reshape(ex, ey, dof)
-        v = jnp.stack([v[i] + update[i] * inverses[i] for i in range(ex)], axis=0)
-
-    final = v.astype(BF16).reshape(ex * ey, dof)
-    traction = dot_nt(traction_ref[...], final).astype(BF16)
-    for owner in range(patches):
-        pull_out[owner] = dot(traction, onehot_elem[owner]).astype(BF16)
-    for j in range(1, patches):
-        pull_first(j, True).start()
-    pulls[s, p] = pull_out[p]
-    fluid_ref[...] = v
-    for j in range(1, patches):
-        pull_first(j, False).wait_recv()
-    for j in range(1, slabs):
-        pull_second(j, True).start()
+        return [v[i] + update[i] * inverses[i] for i in range(ex)]
+
+    def keep(v, k):
+        for i in range(ex):
+            fluid_ref[i] = v[i]
+            if k < SWEEPS:
+                vb[k, i] = v[i].astype(BF16)
+
+    with jax.named_scope("sweep0"):
+        keep(sweep(0, state_ref), 1)
+        send_halos(1)
 
     def scatter(slab, acc):
         for k in range(patches):
@@ -308,19 +549,34 @@
             acc = acc + dot_nt(scaled, onehot_col[slab, :, span])
         return acc
 
-    def arrive(j, carry):
-        point_second(j, False).wait_recv()
-        build_points(slab_peer(j))
-        return carry
-
-    lax.fori_loop(1, slabs, arrive, 0)
+    for i in range(1, patches):
+        pull_arrival(s, patch_peer(i)).wait_recv()
     acc = scatter(s, jnp.zeros((comps * rows, cols), F32))
-
-    def gathered(j, acc):
-        pull_second(j, False).wait_recv()
-        return scatter(slab_peer(j), acc)
-
-    acc = lax.fori_loop(1, slabs, gathered, acc)
+    inner = jnp.minimum(s, slabs - 1 - s)
+
+    def nearest(t):
+        step = lax.div(t + 1, 2)
+        alternate = jnp.where(lax.rem(t, 2) == 1, s + step, s - step)
+        return jnp.where(t <= 2 * inner, alternate, jnp.where(s < slabs - 1 - s, t, slabs - 1 - t))
+
+    def gathered(t, acc):
+        slab = nearest(t)
+        with jax.named_scope("w_point"):
+            remote(points.at[s], points.at[slab], sp2.at[0], rp2.at[slab], (slab, p)).wait_recv()
+        build_points(slab)
+        with jax.named_scope("w_pull"):
+            for i in range(patches):
+                pull_arrival(slab, i).wait_recv()
+        return scatter(slab, acc)
+
+    half = (slabs + 1) // 2
+    with jax.named_scope("gather1"):
+        acc = lax.fori_loop(1, half, gathered, acc)
+    with jax.named_scope("sweep1"):
+        keep(sweep(1, fluid_ref), 2)
+        send_halos(2)
+    with jax.named_scope("gather2"):
+        acc = lax.fori_loop(half, slabs, gathered, acc)
     loads = acc.reshape(comps, rows, cols)
     fresh = [rest_buf[c] + loads[c] * gain_buf[...] for c in range(comps)]
     narrow = jnp.concatenate([x.astype(BF16) for x in fresh], axis=0)
@@ -330,32 +586,47 @@
         hot = onehot_row[s, :, span].astype(F32)
         for c in range(comps):
             picks_out[k, c : c + 1] = jnp.sum(spread[c] * hot, axis=0, keepdims=True)
-    for j in range(1, patches):
-        pick_copy(j, True).start()
+    with jax.named_scope("s_pick"):
+        for j in range(1, patches):
+            pick_copy(j, True).start()
     picks_in[p] = picks_out[p]
     for c in range(comps):
         net_ref[c] = fresh[c]
-    for j in range(1, patches):
-        pick_copy(j, False).wait_recv()
+    with jax.named_scope("sweep2"):
+        keep(sweep(2, fluid_ref), SWEEPS)
+    with jax.named_scope("w_pick"):
+        for j in range(1, patches):
+            pick_copy(j, False).wait_recv()
     for k in range(patches):
         live = lives(k)
         for c in range(comps):
             wall_ref[c, 0, :, k * cap : (k + 1) * cap] = jnp.where(live, picks_in[k, c : c + 1], 0.0)
 
-    for k in range(SWEEPS):
-        pl.when(has_next_s)(lambda: x_up(k).wait_send())
-        pl.when(has_prev_s)(lambda: x_down(k).wait_send())
-        pl.when(has_next_p)(lambda: y_up(k).wait_send())
-        pl.when(has_prev_p)(lambda: y_down(k).wait_send())
-    pl.when(has_next_p)(lambda: d_up().wait_send())
-    pl.when(has_prev_p)(lambda: d_down().wait_send())
-    for j in range(1, patches):
-        point_first(j, True).wait_send()
-        pull_first(j, True).wait_send()
-        pick_copy(j, True).wait_send()
-    for j in range(1, slabs):
-        point_second(j, True).wait_send()
-        pull_second(j, True).wait_send()
+    with jax.named_scope("drain"):
+        for k in range(SWEEPS):
+            pl.when(has_next_s)(lambda: x_up(k).wait_send())
+            pl.when(has_prev_s)(lambda: x_down(k).wait_send())
+            pl.when(has_next_p)(lambda: y_up(k).wait_send())
+            pl.when(has_prev_p)(lambda: y_down(k).wait_send())
+        pl.when(has_next_p)(lambda: d_up().wait_send())
+        pl.when(has_prev_p)(lambda: d_down().wait_send())
+        for n in range(2):
+            pl.when(to_s[n])(lambda: near_copy(n).wait_send())
+            pl.when(to_far[n])(lambda: far_copy(n).wait_send())
+            pl.when(to_p[n])(lambda: side_copy(n).wait_send())
+        for n, m in corners:
+            pl.when(jnp.logical_and(to_s[n], to_p[m]))(lambda: tip_copy(n, m).wait_send())
+        for a, b in around:
+            pl.when(exists(a, b))(lambda: w_copy(a, b).wait_send())
+        for j in range(1, patches):
+            point_first(j, True).wait_send()
+            pick_copy(j, True).wait_send()
+        for j in range(1, slabs):
+            point_second(j, True).wait_send()
+        for j in range(slabs):
+            for i in range(patches):
+                if (j, i) != (0, 0):
+                    pull_copy(j, i).wait_send()
 
 
 def deliver(*refs):
@@ -399,6 +670,16 @@
             pltpu.VMEM((slabs, cols, patches * cap), BF16),
             pltpu.VMEM((comps, rows, cols), F32),
             pltpu.VMEM((rows, cols), F32),
+            pltpu.VMEM((5 * DEEP, ex * ey), BF16),
+            pltpu.VMEM((2, 5 * DEEP, ex * ey), BF16),
+            pltpu.VMEM((8, ex * ey), BF16),
+            pltpu.VMEM((2, 8, ex * ey), BF16),
+            pltpu.VMEM((2, DEEP, dof), BF16),
+            pltpu.VMEM((2, DEEP, dof), BF16),
+            pltpu.VMEM((4, 4, dof), BF16),
+            pltpu.VMEM((4, 4, dof), BF16),
+            pltpu.VMEM((ex, 2 * ey), F32),
+            pltpu.VMEM((9, ex, 2 * ey), F32),
             sem((len(args),)),
             sem((SWEEPS, 2)),
             sem((SWEEPS, 2)),
@@ -410,12 +691,20 @@
             sem((patches,)),
             sem((slabs,)),
             sem((slabs,)),
+            sem((slabs, patches)),
+            sem((slabs, patches)),
             sem((patches,)),
             sem((patches,)),
-            sem((slabs,)),
-            sem((slabs,)),
-            sem((patches,)),
-            sem((patches,)),
+            sem((2,)),
+            sem((2,)),
+            sem((2,)),
+            sem((2,)),
+            sem((2,)),
+            sem((2,)),
+            sem((4,)),
+            sem((4,)),
+            sem((9,)),
+            sem((9,)),
             pltpu.SemaphoreType.REGULAR((max(slabs.bit_length(), 1),)),
         ],
         compiler_params=pltpu.CompilerParams(collective_id=0, has_side_effects=True),

time: 30.4 us -> 23.7 us (0.78)
  Pallas kernels: 29.6 us -> 22.9 us
    pallas_call x1, Pallas kernels: 27.9 us -> 21.3 us  [shards(): pl.pallas_call(functools.partial(kernel, slabs, patches, len(args)), out_...]
where the time goes in v1:
time: 23.7 us; the launch traced here: 23.6 us
  Pallas kernels  22.9 us (97%)
  between operations  0.64 us (3%)
    pallas_call x1, Pallas kernels, shards(): pl.pallas_call(functools.partial(kernel, slabs, patches, len(args)), out_...  21.3 us
    pallas_call x1, Pallas kernels, shards(): pl.pallas_call(deliver, out_shape=tuple((jax.ShapeDtypeStruct(x.shape, x....  1.66 us

profile of v1, /device:TPU:0, one launch (start us, length us, event | category | flops | bytes accessed | tf_op | source)
XLA Modules:
  0.0 23.6 jit_solution(15722690914500388528)
XLA Ops:
  0.6 21.3 %shard_map.148 = (f32[2,64,256]{2,1,0:T(8,128)}, f32[3,64,128]{2,1,0:T(8,128)}, f32[3,1,1,1024]{3,2,1,0:T(1,128)}) custom-call(f32[2,64,256]{2,1,0:T(8,128)} %refs_0_.1, f32[2,64,256]{2,1,0:T(8,128)} %refs_1_.1, f32[2,64]{1,0:T(2,128)} %refs_2_.1, bf16[256,256]{1,0:T(8,128)(2,1)} %refs_3_.1, bf16[256,256]{1,0:T(8,128)(2,1)} %refs_4_.1, ...), custom_call_target="tpu_custom_call" | custom-call | tf_op jit(solution)/shard_map/pallas_call | solution.py:648
  21.9 1.7 %shard_map.149 = (f32[2,64,256]{2,1,0:T(8,128)}, f32[3,64,128]{2,1,0:T(8,128)}, f32[3,1,1,1024]{3,2,1,0:T(1,128)}) custom-call(f32[2,64,256]{2,1,0:T(8,128)} %get-tuple-element.6.refs_0_, f32[3,64,128]{2,1,0:T(8,128)} %get-tuple-element.7.refs_1_, f32[3,1,1,1024]{3,2,1,0:T(1,128)} %get-tuple-element.8.refs_2_), custom_call_target="tpu_custom_call" | custom-call | tf_op jit(solution)/shard_map/pallas_call | solution.py:712

commit v2 on v1

--- a/solution.py
+++ b/solution.py
@@ -347,26 +347,12 @@
         elem = elem_ref[0, :, owner * cap : (owner + 1) * cap]
         hit = (lax.broadcasted_iota(jnp.int32, (wide_lanes, cap), 0) == elem) & lives(owner)
         onehot_elem[owner] = jnp.where(hit, 1.0, 0.0).astype(BF16)
-    for n in range(len(reaches)):
+    if reaches:
         with jax.named_scope("w_reach"):
-            near_wait(n)
-        if n + 1 < len(reaches):
-            near_signal(n + 1)
-        if n == 0:
-            send_halos(0)
-            with jax.named_scope("w_pt1"):
-                for j in range(1, patches):
-                    point_first(j, False).wait_recv()
-            build_points(s)
-    if not reaches:
-        send_halos(0)
-        for j in range(1, patches):
-            point_first(j, False).wait_recv()
-        build_points(s)
-    for j in range(1, slabs):
-        point_second(j, True).start()
-    with jax.named_scope("shell"):
-        shell()
+            near_wait(0)
+        if len(reaches) > 1:
+            near_signal(1)
+    send_halos(0)
     scales = [column(scale_ref[i : i + 1, :]) for i in range(ex)]
     inverses = [1.0 / x for x in scales]
 
@@ -400,6 +386,18 @@
             target = jnp.where(line == n, at, target)
         lanes = lax.broadcasted_iota(jnp.int32, (3 * DEEP, len(span_rows) * wide_lanes), 1)
         return jnp.where(lanes == target, 1.0, 0.0).astype(BF16)
+
+    place_v, place_r = placing(spots_v), placing(spots_r)
+    for n in range(1, len(reaches)):
+        with jax.named_scope("w_reach"):
+            near_wait(n)
+        if n + 1 < len(reaches):
+            near_signal(n + 1)
+    with jax.named_scope("w_pt1"):
+        for j in range(1, patches):
+            point_first(j, False).wait_recv()
+    for j in range(1, slabs):
+        point_second(j, True).start()
 
     with jax.named_scope("w_side"):
         for m in range(2):
@@ -416,8 +414,8 @@
                 for n, m in corners
             ],
         ).astype(BF16)
-        placed_v = dot(dot_nt(words, stack).astype(BF16), placing(spots_v))
-        placed_r = dot(dot_nt(rest, stack).astype(BF16), placing(spots_r))
+        placed_v = dot(dot_nt(words, stack).astype(BF16), place_v)
+        placed_r = dot(dot_nt(rest, stack).astype(BF16), place_r)
 
         def piece(x, r):
             return x[:, (r + ex) * wide_lanes : (r + ex + 1) * wide_lanes]
@@ -549,9 +547,6 @@
             acc = acc + dot_nt(scaled, onehot_col[slab, :, span])
         return acc
 
-    for i in range(1, patches):
-        pull_arrival(s, patch_peer(i)).wait_recv()
-    acc = scatter(s, jnp.zeros((comps * rows, cols), F32))
     inner = jnp.minimum(s, slabs - 1 - s)
 
     def nearest(t):
@@ -559,19 +554,34 @@
         alternate = jnp.where(lax.rem(t, 2) == 1, s + step, s - step)
         return jnp.where(t <= 2 * inner, alternate, jnp.where(s < slabs - 1 - s, t, slabs - 1 - t))
 
-    def gathered(t, acc):
+    def prepared(t, carry):
         slab = nearest(t)
         with jax.named_scope("w_point"):
             remote(points.at[s], points.at[slab], sp2.at[0], rp2.at[slab], (slab, p)).wait_recv()
         build_points(slab)
+        return carry
+
+    def gathered(t, acc):
+        slab = nearest(t)
         with jax.named_scope("w_pull"):
             for i in range(patches):
                 pull_arrival(slab, i).wait_recv()
         return scatter(slab, acc)
 
     half = (slabs + 1) // 2
+    build_points(s)
+    with jax.named_scope("shell"):
+        shell()
+    with jax.named_scope("build1"):
+        lax.fori_loop(1, half, prepared, 0)
+    with jax.named_scope("w_own"):
+        for i in range(1, patches):
+            pull_arrival(s, patch_peer(i)).wait_recv()
+    acc = scatter(s, jnp.zeros((comps * rows, cols), F32))
     with jax.named_scope("gather1"):
         acc = lax.fori_loop(1, half, gathered, acc)
+    with jax.named_scope("build2"):
+        lax.fori_loop(half, slabs, prepared, 0)
     with jax.named_scope("sweep1"):
         keep(sweep(1, fluid_ref), 2)
         send_halos(2)
@@ -648,9 +658,9 @@
     outs = pl.pallas_call(
         functools.partial(kernel, slabs, patches, len(args)),
         out_shape=(
-            jax.ShapeDtypeStruct(state.shape, F32),
-            jax.ShapeDtypeStruct(disp.shape, F32),
-            jax.ShapeDtypeStruct((comps, 1, 1, elem.shape[2]), F32),
+            pltpu.VMEM(state.shape, F32),
+            pltpu.VMEM(disp.shape, F32),
+            pltpu.VMEM((comps, 1, 1, elem.shape[2]), F32),
         ),
         in_specs=[pl.BlockSpec(memory_space=pltpu.HBM)] * len(args),
         out_specs=(vmem, vmem, vmem),
@@ -715,7 +725,7 @@
         in_specs=[vmem] * 3,
         out_specs=(pl.BlockSpec(memory_space=pltpu.HBM),) * 3,
         scratch_shapes=[sem((3,))],
-    )(*outs)
+    )(*[pltpu.with_memory_space_constraint(x, pltpu.VMEM) for x in outs])
 
 
 def solution(mesh):

time: 23.7 us -> 21.9 us (0.924)
  Pallas kernels: 22.9 us -> 21.1 us
    pallas_call x1, Pallas kernels: 1.66 us -> 0.71 us  [shards(): pl.pallas_call(deliver, out_shape=tuple((jax.ShapeDtypeStruct(x.shape, x....]
    pallas_call x1, Pallas kernels: 21.3 us -> 20.4 us  [shards(): pl.pallas_call(functools.partial(kernel, slabs, patches, len(args)), out_...]
where the time goes in v2:
time: 21.9 us; the launch traced here: 21.8 us
  Pallas kernels  21.1 us (96%)
  between operations  0.64 us (3%)
    pallas_call x1, Pallas kernels, shards(): pl.pallas_call(functools.partial(kernel, slabs, patches, len(args)), out_...  20.4 us
    pallas_call x1, Pallas kernels, shards(): pl.pallas_call(deliver, out_shape=tuple((jax.ShapeDtypeStruct(x.shape, x....  0.71 us

profile of v2, /device:TPU:0, one launch (start us, length us, event | category | flops | bytes accessed | tf_op | source)
XLA Modules:
  0.0 21.8 jit_solution(18327390649151789667)
XLA Ops:
  0.6 20.4 %shard_map.148 = (f32[2,64,256]{2,1,0:T(8,128)S(1)}, f32[3,64,128]{2,1,0:T(8,128)S(1)}, f32[3,1,1,1024]{3,2,1,0:T(1,128)S(1)}) custom-call(f32[2,64,256]{2,1,0:T(8,128)} %refs_0_.1, f32[2,64,256]{2,1,0:T(8,128)} %refs_1_.1, f32[2,64]{1,0:T(2,128)} %refs_2_.1, bf16[256,256]{1,0:T(8,128)(2,1)} %refs_3_.1, bf16[256,256]{1,0:T(8,128)(2,1)} %refs_4_.1, ...), custom_call_target="tpu_custom_call" | custom-call | tf_op jit(solution)/shard_map/pallas_call | solution.py:658
  21.0 0.7 %shard_map.149 = (f32[2,64,256]{2,1,0:T(8,128)}, f32[3,64,128]{2,1,0:T(8,128)}, f32[3,1,1,1024]{3,2,1,0:T(1,128)}) custom-call(f32[2,64,256]{2,1,0:T(8,128)S(1)} %get-tuple-element.6.refs_0_, f32[3,64,128]{2,1,0:T(8,128)S(1)} %get-tuple-element.7.refs_1_, f32[3,1,1,1024]{3,2,1,0:T(1,128)S(1)} %get-tuple-element.8.refs_2_), custom_call_target="tpu_custom_call" | custom-call | tf_op jit(solution)/shard_map/pallas_call | solution.py:722

commit v3 on v2

--- a/solution.py
+++ b/solution.py
@@ -12,6 +12,7 @@
 EDGE = 8
 SPARE = 8 * 2**20
 DEEP = 16
+TIP = 8
 LOAD_ORDER = (7, 6, 3, 4, 5, 2, 0, 1, 9, 8, 10, 11, 12)
 MESH = pl.DeviceIdType.MESH
 F32 = jnp.float32
@@ -79,27 +80,35 @@
 def kernel(slabs, patches, args, *refs):
     hbm, refs = refs[:args], refs[args:]
     (fluid_ref, net_ref, wall_ref), refs = refs[:3], refs[3:]
-    staged, refs = refs[:args], refs[args:]
-    (state_ref, rhs_ref, scale_ref, matrix_ref, cx_ref, cy_ref, inverse_ref, traction_ref) = staged[:8]
-    (elem_ref, point_ref, count_ref, disp_ref, stiff_ref) = staged[8:]
+    (state_ref, rhs_ref, scale_ref, matrices, traction_ref, slots, count_ref, nets) = refs[:8]
+    refs = refs[8:]
+    cx_ref, cy_ref, inverse_ref, matrix_ref = (matrices.at[n] for n in range(4))
+    elem_ref, point_ref = slots.at[0], slots.at[1]
     (vb, halo_x, halo_y, halo_d, points, pulls, pull_out, picks_out, picks_in) = refs[:9]
-    (onehot_elem, onehot_row, onehot_col, rest_buf, gain_buf) = refs[9:14]
-    (near_out, near_in, far_out, far_in, side_out, side_in, tip_out, tip_in, w_out, w_in) = refs[14:24]
-    (load_sem, sx, rx, sy, ry, sd, rd, sp1, rp1, sp2, rp2, sq, rq, sw, rw) = refs[24:39]
-    (s_near, r_near, s_far, r_far, s_side, r_side, s_tip, r_tip, s_w, r_w, near_sem) = refs[39:]
-
-    loads_in = [pltpu.make_async_copy(hbm[n], staged[n], load_sem.at[n]) for n in range(args)]
+    (onehot_elem, onehot_row, onehot_col, rest_buf, gain_buf, base_buf) = refs[9:15]
+    (near_out, near_in, far_out, far_in, side_out, side_in, tip_out, tip_in) = refs[15:23]
+    (load_sem, sx, rx, sy, ry, sd, rd, point_sem, rp2, pull_sem, rq, pick_sem) = refs[23:35]
+    (s_near, r_near, s_far, r_far, s_side, r_side, s_tip, r_tip, near_sem) = refs[35:]
+    comps = nets.shape[0] - 1
+    disp_ref, stiff_ref = nets.at[pl.ds(0, comps)], nets.at[comps]
+    homes = (
+        (state_ref, 0), (rhs_ref, 1), (scale_ref, 2), (matrix_ref, 3), (cx_ref, 3), (cy_ref, 3), (inverse_ref, 3),
+        (traction_ref, 4), (elem_ref, 5), (point_ref, 5), (count_ref, 6), (disp_ref, 7), (stiff_ref, 7),
+    )
+
+    loads_in = [pltpu.make_async_copy(hbm[n], homes[n][0], load_sem.at[homes[n][1]]) for n in range(args)]
     for n in LOAD_ORDER:
         loads_in[n].start()
+    groups = (state_ref, rhs_ref, scale_ref, matrices, traction_ref, slots, count_ref, nets)
 
     def ready(*names):
         for n in names:
-            loads_in[n].wait()
+            pltpu.make_async_copy(groups[n], groups[n], load_sem.at[n]).wait()
 
     s = lax.axis_index("slab")
     p = lax.axis_index("patch")
     ex, ey, dof = state_ref.shape
-    comps, rows, cols = disp_ref.shape
+    rows, cols = stiff_ref.shape
     cap = elem_ref.shape[2] // patches
     wide_lanes = ex * ey
 
@@ -164,18 +173,18 @@
         return jnp.clip(p + step, 0, patches - 1)
 
     def x_up(k):
-        return remote(vb.at[k, ex - 1], halo_x.at[k, 0], sx.at[k, 0], rx.at[k, 0], (slab_at(1), p))
+        return remote(vb.at[k, ex - 1], halo_x.at[k, 0], sx.at[0], rx.at[k % 2, 0], (slab_at(1), p))
 
     def x_down(k):
-        return remote(vb.at[k, 0], halo_x.at[k, 1], sx.at[k, 1], rx.at[k, 1], (slab_at(-1), p))
+        return remote(vb.at[k, 0], halo_x.at[k, 1], sx.at[1], rx.at[k % 2, 1], (slab_at(-1), p))
 
     def y_up(k):
         return remote(
-            vb.at[k, :, pl.ds(ey - PACK, PACK)], halo_y.at[k, 0], sy.at[k, 0], ry.at[k, 0], (s, patch_at(1))
+            vb.at[k, :, pl.ds(ey - PACK, PACK)], halo_y.at[k, 0], sy.at[0], ry.at[k % 2, 0], (s, patch_at(1))
         )
 
     def y_down(k):
-        return remote(vb.at[k, :, pl.ds(0, PACK)], halo_y.at[k, 1], sy.at[k, 1], ry.at[k, 1], (s, patch_at(-1)))
+        return remote(vb.at[k, :, pl.ds(0, PACK)], halo_y.at[k, 1], sy.at[1], ry.at[k % 2, 1], (s, patch_at(-1)))
 
     def d_up():
         return remote(disp_ref.at[:, pl.ds(rows - EDGE, EDGE)], halo_d.at[0], sd.at[0], rd.at[0], (s, patch_at(1)))
@@ -195,52 +204,41 @@
     def tip_copy(n, m):
         q = 2 * n + m
         return remote(tip_out.at[q], tip_in.at[q], s_tip.at[q], r_tip.at[q], (slab_at(1 - 2 * n), patch_at(1 - 2 * m)))
-
-    def w_copy(a, b):
-        q = 3 * (1 - a) + 1 - b
-        return remote(w_out, w_in.at[q], s_w.at[q], r_w.at[q], (slab_at(a), patch_at(b)))
 
     to_s, from_s = (has_next_s, has_prev_s), (has_prev_s, has_next_s)
     to_p, from_p = (has_next_p, has_prev_p), (has_prev_p, has_next_p)
     to_far, from_far = (has_far_next, has_far_prev), (has_far_prev, has_far_next)
     corners = [(n, m) for n in range(2) for m in range(2)]
-    around = [(a, b) for a in (-1, 0, 1) for b in (-1, 0, 1) if (a, b) != (0, 0)]
-
-    def exists(a, b):
-        ok_s = {-1: has_prev_s, 0: None, 1: has_next_s}[a]
-        ok_p = {-1: has_prev_p, 0: None, 1: has_next_p}[b]
-        if ok_s is None:
-            return ok_p
-        return ok_s if ok_p is None else jnp.logical_and(ok_s, ok_p)
-
-    def point_first(j, mine):
+    def point_first(j):
         peer = patch_peer(j)
         src = point_ref.at[0, :, pl.ds(pl.multiple_of(peer * cap, cap), cap)]
-        slot = p if mine else peer
-        return remote(src, points.at[s, slot], sp1.at[j], rp1.at[slot], (s, peer))
-
-    def point_second(j, mine):
-        peer = slab_peer(j)
-        slot = s if mine else peer
-        return remote(points.at[s], points.at[slot], sp2.at[j], rp2.at[slot], (peer, p))
+        return remote(src, points.at[s, p], point_sem.at[0], point_sem.at[1], (s, peer))
+
+    def point_second(j):
+        return remote(points.at[s], points.at[s], point_sem.at[2], rp2.at[s], (slab_peer(j), p))
 
     def pull_copy(j, i):
         to = (slab_peer(j), patch_peer(i))
-        return remote(pull_out.at[to[1]], pulls.at[s, p], sq.at[j, i], rq.at[s, p], to)
-
-    def pull_arrival(slab, patch):
-        return remote(pull_out.at[p], pulls.at[slab, patch], sq.at[0, 0], rq.at[slab, patch], (slab, patch))
-
-    def pick_copy(j, mine):
+        here = pl.ds(pl.multiple_of(p * cap, cap), cap)
+        return remote(pull_out.at[to[1]], pulls.at[s, :, here], pull_sem.at[0 if j else 1], rq.at[s], to)
+
+    def pick_copy(j):
         peer = patch_peer(j)
-        slot = p if mine else peer
-        return remote(picks_out.at[peer], picks_in.at[slot], sw.at[j], rw.at[slot], (s, peer))
+        return remote(picks_out.at[peer], picks_in.at[p], pick_sem.at[0], pick_sem.at[1], (s, peer))
+
+    def settle(ref, semaphore):
+        pltpu.make_async_copy(ref, ref, semaphore).wait()
+
+    def halo_sends(k, act):
+        pl.when(has_next_s)(lambda: act(x_up(k)))
+        pl.when(has_prev_s)(lambda: act(x_down(k)))
+        pl.when(has_next_p)(lambda: act(y_up(k)))
+        pl.when(has_prev_p)(lambda: act(y_down(k)))
 
     def send_halos(k):
-        pl.when(has_next_s)(lambda: x_up(k).start())
-        pl.when(has_prev_s)(lambda: x_down(k).start())
-        pl.when(has_next_p)(lambda: y_up(k).start())
-        pl.when(has_prev_p)(lambda: y_down(k).start())
+        if k > 0:
+            halo_sends(k - 1, lambda copy: copy.wait_send())
+        halo_sends(k, lambda copy: copy.start())
 
     def build_points(slab):
         for k in range(patches):
@@ -275,22 +273,29 @@
             rest_buf[c] = disp_ref[c] - stiff_ref[...] * full * gain
 
     with jax.named_scope("words"):
-        ready(7, 6, 4, 3, 5)
+        ready(4, 3)
         words, rest = make_words(
             traction_ref[...], inverse_ref[...], matrix_ref[...], cx_ref[...], cy_ref[...]
         )
     ready(2)
-    w_out[...] = blank(*w_out.shape)
-    w_out[:, 0:ey] = 1.0 / scale_ref[...]
+    flat = 1.0 / scale_ref[...]
+    w_own = jnp.concatenate([flat, blank(ex, wide_lanes - ey)], axis=1)
     ready(0)
     rounded0 = state_ref[...].astype(BF16)
     vb[0] = rounded0
     ready(1)
     wet = rhs_ref[...].astype(BF16)
+    lane = lax.broadcasted_iota(jnp.int32, (1, wide_lanes), 1)
+    low_half = lane < ey
+    tail_half = lane < ey + ey // 2
+    w_lines = jnp.concatenate([w_own] + [blank(ex, wide_lanes)] * (dof // wide_lanes - 1), axis=1)
     with jax.named_scope("project"):
         own_v = dot_nt(words, rounded0.reshape(wide_lanes, dof))
         own_r = dot_nt(rest, wet.reshape(wide_lanes, dof))
-        spare = join(blank(2 * DEEP - comps - 1, wide_lanes), own_r[2 * DEEP : 2 * DEEP + comps], blank(1, wide_lanes))
+        packed = jnp.where(low_half, w_own[0:1], pltpu.roll(w_own[1:2], ey, 1))
+        spare = join(
+            blank(2 * DEEP - comps - 1, wide_lanes), own_r[2 * DEEP : 2 * DEEP + comps], packed
+        )
         near_out[...] = join(
             own_v[0:DEEP], own_v[2 * DEEP : 4 * DEEP] + spare, own_v[4 * DEEP : 5 * DEEP], own_r[0:DEEP]
         ).astype(BF16)
@@ -306,7 +311,7 @@
             edge = [ey - 1 - j if m == 0 else j for j in range(SWEEPS)]
             lines = [state_at(i, c) for i in range(ex) for c in edge]
             lines += [rhs_at(i, c) for i in range(ex) for c in edge[: SWEEPS - 1]]
-            side_out[m] = join(*lines, blank(DEEP - len(lines), dof)).astype(BF16)
+            side_out[m] = join(*lines, w_lines, blank(DEEP - ex - len(lines), dof)).astype(BF16)
             for n in range(2):
                 order = [ex - 1, ex - 2] if n == 0 else [0, 1]
                 tip_out[2 * n + m] = join(
@@ -314,29 +319,29 @@
                     state_at(order[0], edge[1]),
                     state_at(order[1], edge[0]),
                     rhs_at(order[0], edge[0]),
+                    w_lines[order[0] : order[0] + 1],
+                    blank(TIP - 5, dof),
                 ).astype(BF16)
 
     with jax.named_scope("w_barrier"):
         pl.semaphore_wait(barrier, awaited)
-    for n in range(2):
-        pl.when(to_s[n])(lambda: near_copy(n).start())
     for n, m in corners:
         pl.when(jnp.logical_and(to_s[n], to_p[m]))(lambda: tip_copy(n, m).start())
     for n in range(2):
-        pl.when(to_far[n])(lambda: far_copy(n).start())
+        pl.when(to_s[n])(lambda: near_copy(n).start())
     for m in range(2):
         pl.when(to_p[m])(lambda: side_copy(m).start())
-    for a, b in around:
-        pl.when(exists(a, b))(lambda: w_copy(a, b).start())
+    for n in range(2):
+        pl.when(to_far[n])(lambda: far_copy(n).start())
     if reaches:
         near_signal(0)
-    ready(9)
+    ready(5)
     for j in range(1, patches):
-        point_first(j, True).start()
-    ready(11)
+        point_first(j).start()
+    ready(7)
     pl.when(has_next_p)(lambda: d_up().start())
     pl.when(has_prev_p)(lambda: d_down().start())
-    ready(8, 10, 12)
+    ready(6)
     for owner in range(patches):
 
         @pl.when(p == owner)
@@ -356,14 +361,21 @@
     scales = [column(scale_ref[i : i + 1, :]) for i in range(ex)]
     inverses = [1.0 / x for x in scales]
 
-    lane = lax.broadcasted_iota(jnp.int32, (1, wide_lanes), 1)
-    low_half = lane < ey
-    tail_half = lane < ey + ey // 2
+    def prelude(k):
+        own = dot(vb[k].reshape(ex * ey, dof), matrix_ref[...]).reshape(ex, ey, dof)
+        for i in range(ex):
+            base_buf[i] = rhs_ref[i] - scales[i] * own[i]
+
+    with jax.named_scope("shell"):
+        shell()
+    with jax.named_scope("prelude"):
+        prelude(0)
 
     def halves(x):
         return jnp.where(low_half, x, 0.0), jnp.where(low_half, pltpu.roll(x, ey, 1), 0.0)
 
     span_rows = list(range(-ex, 2 * ex))
+    stack_rows = 2 * DEEP + 4 * TIP
     spots_v, spots_r = [], []
     for m in range(2):
         def spot(r, j):
@@ -375,63 +387,46 @@
             spots_r += [(first + j, spot(i, j)) for j in range(1, SWEEPS)]
         for n in range(2):
             r1, r2 = (-1, -2) if n == 0 else (ex, ex + 1)
-            first = 2 * DEEP + 4 * (2 * n + m)
+            first = 2 * DEEP + TIP * (2 * n + m)
             spots_v += [(first, spot(r1, 1)), (first + 1, spot(r1, 2)), (first + 2, spot(r2, 1))]
             spots_r += [(first + 3, spot(r1, 1))]
 
     def placing(spots):
-        line = lax.broadcasted_iota(jnp.int32, (3 * DEEP, 1), 0)
-        target = jnp.full((3 * DEEP, 1), -1, jnp.int32)
+        line = lax.broadcasted_iota(jnp.int32, (stack_rows, 1), 0)
+        target = jnp.full((stack_rows, 1), -1, jnp.int32)
         for n, at in spots:
             target = jnp.where(line == n, at, target)
-        lanes = lax.broadcasted_iota(jnp.int32, (3 * DEEP, len(span_rows) * wide_lanes), 1)
+        lanes = lax.broadcasted_iota(jnp.int32, (stack_rows, len(span_rows) * wide_lanes), 1)
         return jnp.where(lanes == target, 1.0, 0.0).astype(BF16)
 
     place_v, place_r = placing(spots_v), placing(spots_r)
-    for n in range(1, len(reaches)):
-        with jax.named_scope("w_reach"):
-            near_wait(n)
-        if n + 1 < len(reaches):
-            near_signal(n + 1)
-    with jax.named_scope("w_pt1"):
-        for j in range(1, patches):
-            point_first(j, False).wait_recv()
-    for j in range(1, slabs):
-        point_second(j, True).start()
-
     with jax.named_scope("w_side"):
         for m in range(2):
             pl.when(from_p[m])(lambda: side_copy(m).wait_recv())
-        for a, b in around:
-            pl.when(exists(-a, -b))(lambda: w_copy(a, b).wait_recv())
         for n, m in corners:
             pl.when(jnp.logical_and(from_s[n], from_p[m]))(lambda: tip_copy(n, m).wait_recv())
     with jax.named_scope("place"):
-        stack = join(
-            *[jnp.where(from_p[m], side_in[m].astype(F32), 0.0) for m in range(2)],
-            *[
-                jnp.where(jnp.logical_and(from_s[n], from_p[m]), tip_in[2 * n + m].astype(F32), 0.0)
-                for n, m in corners
-            ],
-        ).astype(BF16)
+        sides = [jnp.where(from_p[m], side_in[m].astype(F32), 0.0) for m in range(2)]
+        tips = [
+            jnp.where(jnp.logical_and(from_s[n], from_p[m]), tip_in[2 * n + m].astype(F32), 0.0) for n, m in corners
+        ]
+        stack = join(*sides, *tips).astype(BF16)
         placed_v = dot(dot_nt(words, stack).astype(BF16), place_v)
         placed_r = dot(dot_nt(rest, stack).astype(BF16), place_r)
 
         def piece(x, r):
             return x[:, (r + ex) * wide_lanes : (r + ex + 1) * wide_lanes]
 
-        def weight(a, b):
-            if (a, b) == (0, 0):
-                return w_out[...]
-            return jnp.where(exists(a, b), w_in[3 * (a + 1) + b + 1], 0.0)
-
+        def framed(middle, before, after):
+            before, after = pltpu.roll(before, ey, 1), pltpu.roll(after, ey, 1)
+            return jnp.where(low_half, middle, jnp.where(tail_half, after, before))
+
+        w_at = ex * (2 * SWEEPS - 1)
         w_rows = {}
-        for a in (-1, 0, 1):
-            middle = weight(a, 0)
-            before, after = pltpu.roll(weight(a, -1), ey, 1), pltpu.roll(weight(a, 1), ey, 1)
-            both = jnp.where(low_half, middle, jnp.where(tail_half, after, before))
-            for i in range(ex):
-                w_rows[a * ex + i] = both[i : i + 1]
+        for i in range(ex):
+            ends = [sides[m][w_at + i : w_at + i + 1, :wide_lanes] for m in range(2)]
+            w_rows[i] = framed(w_own[i : i + 1], *ends)
+        w_tips = [[tips[2 * n + m][4:5, :wide_lanes] for m in range(2)] for n in range(2)]
 
     with jax.named_scope("w_near"):
         for n in range(2):
@@ -456,6 +451,9 @@
                 by_y[r] = half[3 * DEEP : 4 * DEEP] + edge_v[4 * DEEP : 5 * DEEP]
                 by_r2[r] = half[4 * DEEP : 5 * DEEP] + edge_r[0:DEEP]
                 by_r1[r] = half[3 * DEEP - comps - 1 : 3 * DEEP - 1]
+                w_rows[r] = half[3 * DEEP - 1 : 3 * DEEP]
+                if r in (-1, ex):
+                    w_rows[r] = framed(w_rows[r], *w_tips[n])
             beyond = halves(jnp.where(from_far[n], far_in[n].astype(F32), 0.0))[1 - n]
             by_x[-ex - 1 if n == 0 else 2 * ex] = join(beyond, blank(DEEP - 8, wide_lanes))
 
@@ -487,17 +485,29 @@
         traction = jnp.where(low_half, drawn[0], pltpu.roll(drawn[1], ey, 1)).astype(BF16)
         for owner in range(patches):
             pull_out[owner] = dot(traction, onehot_elem[owner]).astype(BF16)
+    for n in range(1, len(reaches)):
+        with jax.named_scope("w_reach"):
+            near_wait(n)
+        if n + 1 < len(reaches):
+            near_signal(n + 1)
+    with jax.named_scope("w_pt1"):
+        settle(points.at[s, pl.ds(0, patches - 1)], point_sem.at[1])
+    for j in range(1, slabs):
+        point_second(j).start()
     with jax.named_scope("s_pull"):
         for j in sorted(range(slabs), key=lambda j: -min(j, slabs - j)):
             for i in range(patches):
                 if (j, i) != (0, 0):
                     pull_copy(j, i).start()
-    pulls[s, p] = pull_out[p]
+    for owner in range(patches):
+
+        @pl.when(p == owner)
+        def _():
+            pulls[s, :, owner * cap : (owner + 1) * cap] = pull_out[owner]
+
 
     def sweep(k, v):
-        rounded = rounded0 if k == 0 else vb[k]
-        own = dot(rounded.reshape(ex * ey, dof), matrix_ref[...]).reshape(ex, ey, dof)
-        base = [rhs_ref[i] - scales[i] * own[i] for i in range(ex)]
+        rounded = vb[k]
         wide = rounded.astype(F32)
         with jax.named_scope("w_halo"):
             pl.when(has_prev_p)(lambda: y_up(k).wait_recv())
@@ -524,7 +534,7 @@
             along_x.append((below + above).astype(BF16))
         side_x = dot(jnp.concatenate(along_x, axis=0), cx_ref[...])
         side = (side_x + side_y).reshape(ex, ey, dof)
-        residue = jnp.concatenate([(base[i] + side[i]).astype(BF16) for i in range(ex)], axis=0)
+        residue = jnp.concatenate([(base_buf[i] + side[i]).astype(BF16) for i in range(ex)], axis=0)
         update = dot(residue, inverse_ref[...]).reshape(ex, ey, dof)
         return [v[i] + update[i] * inverses[i] for i in range(ex)]
 
@@ -537,15 +547,13 @@
     with jax.named_scope("sweep0"):
         keep(sweep(0, state_ref), 1)
         send_halos(1)
+        prelude(1)
 
     def scatter(slab, acc):
-        for k in range(patches):
-            span = pl.ds(k * cap, cap)
-            hot = onehot_row[slab, :, span]
-            value = pulls[slab, k]
-            scaled = jnp.concatenate([hot * value[c : c + 1] for c in range(comps)], axis=0)
-            acc = acc + dot_nt(scaled, onehot_col[slab, :, span])
-        return acc
+        hot = onehot_row[slab]
+        value = pulls[slab]
+        scaled = jnp.concatenate([hot * value[c : c + 1] for c in range(comps)], axis=0)
+        return acc + dot_nt(scaled, onehot_col[slab])
 
     inner = jnp.minimum(s, slabs - 1 - s)
 
@@ -557,26 +565,22 @@
     def prepared(t, carry):
         slab = nearest(t)
         with jax.named_scope("w_point"):
-            remote(points.at[s], points.at[slab], sp2.at[0], rp2.at[slab], (slab, p)).wait_recv()
+            settle(points.at[slab], rp2.at[slab])
         build_points(slab)
         return carry
 
     def gathered(t, acc):
         slab = nearest(t)
         with jax.named_scope("w_pull"):
-            for i in range(patches):
-                pull_arrival(slab, i).wait_recv()
+            settle(pulls.at[slab], rq.at[slab])
         return scatter(slab, acc)
 
     half = (slabs + 1) // 2
     build_points(s)
-    with jax.named_scope("shell"):
-        shell()
     with jax.named_scope("build1"):
         lax.fori_loop(1, half, prepared, 0)
     with jax.named_scope("w_own"):
-        for i in range(1, patches):
-            pull_arrival(s, patch_peer(i)).wait_recv()
+        settle(pulls.at[s, :, pl.ds(0, (patches - 1) * cap)], rq.at[s])
     acc = scatter(s, jnp.zeros((comps * rows, cols), F32))
     with jax.named_scope("gather1"):
         acc = lax.fori_loop(1, half, gathered, acc)
@@ -598,26 +602,22 @@
             picks_out[k, c : c + 1] = jnp.sum(spread[c] * hot, axis=0, keepdims=True)
     with jax.named_scope("s_pick"):
         for j in range(1, patches):
-            pick_copy(j, True).start()
+            pick_copy(j).start()
     picks_in[p] = picks_out[p]
     for c in range(comps):
         net_ref[c] = fresh[c]
     with jax.named_scope("sweep2"):
+        prelude(2)
         keep(sweep(2, fluid_ref), SWEEPS)
     with jax.named_scope("w_pick"):
-        for j in range(1, patches):
-            pick_copy(j, False).wait_recv()
+        settle(picks_in.at[pl.ds(0, patches - 1)], pick_sem.at[1])
     for k in range(patches):
         live = lives(k)
         for c in range(comps):
             wall_ref[c, 0, :, k * cap : (k + 1) * cap] = jnp.where(live, picks_in[k, c : c + 1], 0.0)
 
     with jax.named_scope("drain"):
-        for k in range(SWEEPS):
-            pl.when(has_next_s)(lambda: x_up(k).wait_send())
-            pl.when(has_prev_s)(lambda: x_down(k).wait_send())
-            pl.when(has_next_p)(lambda: y_up(k).wait_send())
-            pl.when(has_prev_p)(lambda: y_down(k).wait_send())
+        halo_sends(SWEEPS - 1, lambda copy: copy.wait_send())
         pl.when(has_next_p)(lambda: d_up().wait_send())
         pl.when(has_prev_p)(lambda: d_down().wait_send())
         for n in range(2):
@@ -626,17 +626,11 @@
             pl.when(to_p[n])(lambda: side_copy(n).wait_send())
         for n, m in corners:
             pl.when(jnp.logical_and(to_s[n], to_p[m]))(lambda: tip_copy(n, m).wait_send())
-        for a, b in around:
-            pl.when(exists(a, b))(lambda: w_copy(a, b).wait_send())
-        for j in range(1, patches):
-            point_first(j, True).wait_send()
-            pick_copy(j, True).wait_send()
-        for j in range(1, slabs):
-            point_second(j, True).wait_send()
-        for j in range(slabs):
-            for i in range(patches):
-                if (j, i) != (0, 0):
-                    pull_copy(j, i).wait_send()
+        settle(points.at[s, pl.ds(0, patches - 1)], point_sem.at[0])
+        settle(points.at[pl.ds(0, slabs - 1)], point_sem.at[2])
+        settle(pulls.at[pl.ds(0, slabs - 1)], pull_sem.at[0])
+        settle(pulls.at[s, :, pl.ds(0, (patches - 1) * cap)], pull_sem.at[1])
+        settle(picks_in.at[pl.ds(0, patches - 1)], pick_sem.at[0])
 
 
 def deliver(*refs):
@@ -664,14 +658,19 @@
         ),
         in_specs=[pl.BlockSpec(memory_space=pltpu.HBM)] * len(args),
         out_specs=(vmem, vmem, vmem),
-        scratch_shapes=[pltpu.VMEM(x.shape, x.dtype) for x in args]
+        scratch_shapes=[pltpu.VMEM(x.shape, x.dtype) for x in args[:3]]
         + [
+            pltpu.VMEM((4,) + args[3].shape, BF16),
+            pltpu.VMEM(args[7].shape, BF16),
+            pltpu.VMEM((2,) + elem.shape, jnp.int32),
+            pltpu.VMEM(args[10].shape, jnp.int32),
+            pltpu.VMEM((comps + 1, rows, cols), F32),
             pltpu.VMEM((SWEEPS, ex, ey, dof), BF16),
             pltpu.VMEM((SWEEPS, 2, ey, dof), BF16),
             pltpu.VMEM((SWEEPS, 2, ex, PACK, dof), BF16),
             pltpu.VMEM((2, comps, EDGE, cols), F32),
             pltpu.VMEM((slabs, patches, 1, cap), jnp.int32),
-            pltpu.VMEM((slabs, patches, comps, cap), BF16),
+            pltpu.VMEM((slabs, comps, patches * cap), BF16),
             pltpu.VMEM((patches, comps, cap), BF16),
             pltpu.VMEM((patches, comps, cap), F32),
             pltpu.VMEM((patches, comps, cap), F32),
@@ -680,31 +679,27 @@
             pltpu.VMEM((slabs, cols, patches * cap), BF16),
             pltpu.VMEM((comps, rows, cols), F32),
             pltpu.VMEM((rows, cols), F32),
+            pltpu.VMEM(state.shape, F32),
             pltpu.VMEM((5 * DEEP, ex * ey), BF16),
             pltpu.VMEM((2, 5 * DEEP, ex * ey), BF16),
             pltpu.VMEM((8, ex * ey), BF16),
             pltpu.VMEM((2, 8, ex * ey), BF16),
             pltpu.VMEM((2, DEEP, dof), BF16),
             pltpu.VMEM((2, DEEP, dof), BF16),
-            pltpu.VMEM((4, 4, dof), BF16),
-            pltpu.VMEM((4, 4, dof), BF16),
-            pltpu.VMEM((ex, 2 * ey), F32),
-            pltpu.VMEM((9, ex, 2 * ey), F32),
-            sem((len(args),)),
-            sem((SWEEPS, 2)),
-            sem((SWEEPS, 2)),
-            sem((SWEEPS, 2)),
-            sem((SWEEPS, 2)),
-            sem((2,)),
-            sem((2,)),
-            sem((patches,)),
-            sem((patches,)),
+            pltpu.VMEM((4, TIP, dof), BF16),
+            pltpu.VMEM((4, TIP, dof), BF16),
+            sem((8,)),
+            sem((2,)),
+            sem((2, 2)),
+            sem((2,)),
+            sem((2, 2)),
+            sem((2,)),
+            sem((2,)),
+            sem((3,)),
             sem((slabs,)),
+            sem((2,)),
             sem((slabs,)),
-            sem((slabs, patches)),
-            sem((slabs, patches)),
-            sem((patches,)),
-            sem((patches,)),
+            sem((2,)),
             sem((2,)),
             sem((2,)),
             sem((2,)),
@@ -713,9 +708,7 @@
             sem((2,)),
             sem((4,)),
             sem((4,)),
-            sem((9,)),
-            sem((9,)),
-            pltpu.SemaphoreType.REGULAR((max(slabs.bit_length(), 1),)),
+            pltpu.SemaphoreType.REGULAR((max(slabs.bit_length() - 2, 1),)),
         ],
         compiler_params=pltpu.CompilerParams(collective_id=0, has_side_effects=True),
     )(*args)

time: 21.9 us -> 21.1 us (0.963)
  Pallas kernels: 21.1 us -> 20.3 us
    pallas_call x1, Pallas kernels: 20.4 us -> 19.6 us  [shards(): pl.pallas_call(functools.partial(kernel, slabs, patches, len(args)), out_...]
where the time goes in v3:
time: 21.1 us; the launch traced here: 21 us
  Pallas kernels  20.3 us (96%)
  between operations  0.64 us (3%)
    pallas_call x1, Pallas kernels, shards(): pl.pallas_call(functools.partial(kernel, slabs, patches, len(args)), out_...  19.6 us
    pallas_call x1, Pallas kernels, shards(): pl.pallas_call(deliver, out_shape=tuple((jax.ShapeDtypeStruct(x.shape, x....  0.71 us

profile of v3, /device:TPU:0, one launch (start us, length us, event | category | flops | bytes accessed | tf_op | source)
XLA Modules:
  0.0 21.0 jit_solution(13891929825880415010)
XLA Ops:
  0.6 19.6 %shard_map.148 = (f32[2,64,256]{2,1,0:T(8,128)S(1)}, f32[3,64,128]{2,1,0:T(8,128)S(1)}, f32[3,1,1,1024]{3,2,1,0:T(1,128)S(1)}) custom-call(f32[2,64,256]{2,1,0:T(8,128)} %refs_0_.1, f32[2,64,256]{2,1,0:T(8,128)} %refs_1_.1, f32[2,64]{1,0:T(2,128)} %refs_2_.1, bf16[256,256]{1,0:T(8,128)(2,1)} %refs_3_.1, bf16[256,256]{1,0:T(8,128)(2,1)} %refs_4_.1, ...), custom_call_target="tpu_custom_call" | custom-call | tf_op jit(solution)/shard_map/pallas_call | solution.py:652
  20.3 0.7 %shard_map.149 = (f32[2,64,256]{2,1,0:T(8,128)}, f32[3,64,128]{2,1,0:T(8,128)}, f32[3,1,1,1024]{3,2,1,0:T(1,128)}) custom-call(f32[2,64,256]{2,1,0:T(8,128)S(1)} %get-tuple-element.6.refs_0_, f32[3,64,128]{2,1,0:T(8,128)S(1)} %get-tuple-element.7.refs_1_, f32[3,1,1,1024]{3,2,1,0:T(1,128)S(1)} %get-tuple-element.8.refs_2_), custom_call_target="tpu_custom_call" | custom-call | tf_op jit(solution)/shard_map/pallas_call | solution.py:715

commit v4 on v3

--- a/solution.py
+++ b/solution.py
@@ -86,9 +86,10 @@
     elem_ref, point_ref = slots.at[0], slots.at[1]
     (vb, halo_x, halo_y, halo_d, points, pulls, pull_out, picks_out, picks_in) = refs[:9]
     (onehot_elem, onehot_row, onehot_col, rest_buf, gain_buf, base_buf) = refs[9:15]
-    (near_out, near_in, far_out, far_in, side_out, side_in, tip_out, tip_in) = refs[15:23]
-    (load_sem, sx, rx, sy, ry, sd, rd, point_sem, rp2, pull_sem, rq, pick_sem) = refs[23:35]
-    (s_near, r_near, s_far, r_far, s_side, r_side, s_tip, r_tip, near_sem) = refs[35:]
+    (near_out, near_in, far_out, far_in, side_out, tip_out, rim) = refs[15:22]
+    (load_sem, rx, ry, sd, rd, point_sem, rp2, pull_sem, rq, pick_sem) = refs[22:32]
+    (s_near, r_near, s_far, r_far, s_side, r_side, s_tip, r_tip, near_sem) = refs[32:]
+    sx, sy = s_near, s_side
     comps = nets.shape[0] - 1
     disp_ref, stiff_ref = nets.at[pl.ds(0, comps)], nets.at[comps]
     homes = (
@@ -192,6 +193,13 @@
     def d_down():
         return remote(disp_ref.at[:, pl.ds(0, EDGE)], halo_d.at[1], sd.at[1], rd.at[1], (s, patch_at(-1)))
 
+    shift = ey - TIP
+    side_base = (shift, 0)
+    tip_base = [(DEEP + TIP * n + ey, DEEP + TIP * n) for n in range(2)]
+
+    side_w = ex * (2 * SWEEPS - 1)
+    side_v = SWEEPS + 2
+
     def near_copy(n):
         return remote(near_out, near_in.at[n], s_near.at[n], r_near.at[n], (slab_at(1 - 2 * n), p))
 
@@ -199,11 +207,11 @@
         return remote(far_out, far_in.at[n], s_far.at[n], r_far.at[n], (slab_at(2 - 4 * n), p))
 
     def side_copy(n):
-        return remote(side_out.at[n], side_in.at[n], s_side.at[n], r_side.at[n], (s, patch_at(1 - 2 * n)))
+        return remote(side_out.at[n], rim.at[pl.ds(side_base[n], DEEP)], s_side.at[n], r_side.at[n], (s, patch_at(1 - 2 * n)))
 
     def tip_copy(n, m):
         q = 2 * n + m
-        return remote(tip_out.at[q], tip_in.at[q], s_tip.at[q], r_tip.at[q], (slab_at(1 - 2 * n), patch_at(1 - 2 * m)))
+        return remote(tip_out.at[q], rim.at[pl.ds(tip_base[n][m], TIP)], s_tip.at[q], r_tip.at[q], (slab_at(1 - 2 * n), patch_at(1 - 2 * m)))
 
     to_s, from_s = (has_next_s, has_prev_s), (has_prev_s, has_next_s)
     to_p, from_p = (has_next_p, has_prev_p), (has_prev_p, has_next_p)
@@ -232,12 +240,19 @@
     def halo_sends(k, act):
         pl.when(has_next_s)(lambda: act(x_up(k)))
         pl.when(has_prev_s)(lambda: act(x_down(k)))
-        pl.when(has_next_p)(lambda: act(y_up(k)))
-        pl.when(has_prev_p)(lambda: act(y_down(k)))
+        if k > 0:
+            pl.when(has_next_p)(lambda: act(y_up(k)))
+            pl.when(has_prev_p)(lambda: act(y_down(k)))
 
     def send_halos(k):
-        if k > 0:
+        if k == 0:
+            for n in range(2):
+                pl.when(to_s[n])(lambda: near_copy(n).wait_send())
+        else:
             halo_sends(k - 1, lambda copy: copy.wait_send())
+        if k == 1:
+            for n in range(2):
+                pl.when(to_p[n])(lambda: side_copy(n).wait_send())
         halo_sends(k, lambda copy: copy.start())
 
     def build_points(slab):
@@ -272,8 +287,9 @@
             full = (laplace(bend) + 4.0 * bend)[EDGE : EDGE + rows]
             rest_buf[c] = disp_ref[c] - stiff_ref[...] * full * gain
 
+    with jax.named_scope("w_mat"):
+        ready(4, 3)
     with jax.named_scope("words"):
-        ready(4, 3)
         words, rest = make_words(
             traction_ref[...], inverse_ref[...], matrix_ref[...], cx_ref[...], cy_ref[...]
         )
@@ -308,20 +324,27 @@
             return rhs_ref[i, c : c + 1]
 
         for m in range(2):
-            edge = [ey - 1 - j if m == 0 else j for j in range(SWEEPS)]
-            lines = [state_at(i, c) for i in range(ex) for c in edge]
-            lines += [rhs_at(i, c) for i in range(ex) for c in edge[: SWEEPS - 1]]
-            side_out[m] = join(*lines, w_lines, blank(DEEP - ex - len(lines), dof)).astype(BF16)
+            close = [ey - 1 - j if m == 0 else j for j in range(SWEEPS)]
+            if m == 1:
+                side = [state_at(i, c) for i in range(ex) for c in close]
+                side += [rhs_at(i, c) for i in range(ex) for c in close[: SWEEPS - 1]]
+                side += [w_lines, blank(DEEP - side_w - ex, dof)]
+            else:
+                side = [w_lines, blank(side_v - ex, dof)]
+                side += [state_at(i, c) for i in range(ex) for c in close[::-1]]
+                side += [blank(1, dof)]
+                side += [rhs_at(i, c) for i in range(ex) for c in close[: SWEEPS - 1][::-1]]
+            side_out[m] = join(*side).astype(BF16)
             for n in range(2):
-                order = [ex - 1, ex - 2] if n == 0 else [0, 1]
-                tip_out[2 * n + m] = join(
-                    state_at(order[0], edge[0]),
-                    state_at(order[0], edge[1]),
-                    state_at(order[1], edge[0]),
-                    rhs_at(order[0], edge[0]),
-                    w_lines[order[0] : order[0] + 1],
-                    blank(TIP - 5, dof),
-                ).astype(BF16)
+                r1, r2 = (ex - 1, ex - 2) if n == 0 else (0, 1)
+                near2 = [state_at(r1, close[0]), state_at(r1, close[1])]
+                last = [state_at(r2, close[0]), rhs_at(r1, close[0])]
+                weigh = w_lines[r1 : r1 + 1]
+                if m == 1:
+                    tip = [weigh, blank(1, dof), *near2, *last, blank(TIP - 6, dof)]
+                else:
+                    tip = [*near2[::-1], blank(1, dof), *last, weigh, blank(TIP - 6, dof)]
+                tip_out[2 * n + m] = join(*tip).astype(BF16)
 
     with jax.named_scope("w_barrier"):
         pl.semaphore_wait(barrier, awaited)
@@ -350,8 +373,10 @@
 
     for owner in range(patches):
         elem = elem_ref[0, :, owner * cap : (owner + 1) * cap]
-        hit = (lax.broadcasted_iota(jnp.int32, (wide_lanes, cap), 0) == elem) & lives(owner)
-        onehot_elem[owner] = jnp.where(hit, 1.0, 0.0).astype(BF16)
+        for i in range(ex):
+            line = lax.broadcasted_iota(jnp.int32, (wide_lanes, cap), 0)
+            hit = (line + i * ey == elem) & (line < ey) & lives(owner)
+            onehot_elem[owner, i] = jnp.where(hit, 1.0, 0.0).astype(BF16)
     if reaches:
         with jax.named_scope("w_reach"):
             near_wait(0)
@@ -375,58 +400,76 @@
         return jnp.where(low_half, x, 0.0), jnp.where(low_half, pltpu.roll(x, ey, 1), 0.0)
 
     span_rows = list(range(-ex, 2 * ex))
-    stack_rows = 2 * DEEP + 4 * TIP
-    spots_v, spots_r = [], []
-    for m in range(2):
-        def spot(r, j):
-            return (r + ex) * wide_lanes + (wide_lanes - j if m == 0 else ey + j - 1)
-
-        for i in range(ex):
-            spots_v += [(m * DEEP + i * SWEEPS + j - 1, spot(i, j)) for j in range(1, SWEEPS + 1)]
-            first = m * DEEP + ex * SWEEPS + i * (SWEEPS - 1) - 1
-            spots_r += [(first + j, spot(i, j)) for j in range(1, SWEEPS)]
-        for n in range(2):
-            r1, r2 = (-1, -2) if n == 0 else (ex, ex + 1)
-            first = 2 * DEEP + TIP * (2 * n + m)
-            spots_v += [(first, spot(r1, 1)), (first + 1, spot(r1, 2)), (first + 2, spot(r2, 1))]
-            spots_r += [(first + 3, spot(r1, 1))]
-
-    def placing(spots):
-        line = lax.broadcasted_iota(jnp.int32, (stack_rows, 1), 0)
-        target = jnp.full((stack_rows, 1), -1, jnp.int32)
-        for n, at in spots:
-            target = jnp.where(line == n, at, target)
-        lanes = lax.broadcasted_iota(jnp.int32, (stack_rows, len(span_rows) * wide_lanes), 1)
-        return jnp.where(lanes == target, 1.0, 0.0).astype(BF16)
-
-    place_v, place_r = placing(spots_v), placing(spots_r)
+
+    def between(low, high):
+        return (lane >= low) & (lane < high)
+
+    def frame_mask(n, reach):
+        right, left = has_next_p, has_prev_p
+        if n is not None:
+            right, left = jnp.logical_and(right, from_s[n]), jnp.logical_and(left, from_s[n])
+        right, left = jnp.where(right, 1, 0), jnp.where(left, 1, 0)
+        ahead, behind = between(ey, ey + reach), between(wide_lanes - reach, wide_lanes)
+        return jnp.where(ahead, right, jnp.where(behind, left, 0)) > 0
+
+    masks = {(n, reach): frame_mask(n, reach) for n in (None, 0, 1) for reach in range(1, SWEEPS + 1)}
+
+    def framing(x, source, mask):
+        return jnp.where(mask, pltpu.roll(x, (ey - source) % wide_lanes, 1), 0.0)
+
+    with jax.named_scope("halves"):
+        own_rows = list(zip(halves(own_v), halves(own_r)))
     with jax.named_scope("w_side"):
         for m in range(2):
             pl.when(from_p[m])(lambda: side_copy(m).wait_recv())
         for n, m in corners:
             pl.when(jnp.logical_and(from_s[n], from_p[m]))(lambda: tip_copy(n, m).wait_recv())
+    for n in range(1, len(reaches)):
+        with jax.named_scope("w_reach"):
+            near_wait(n)
+        if n + 1 < len(reaches):
+            near_signal(n + 1)
+    with jax.named_scope("w_pt1"):
+        settle(points.at[s, pl.ds(0, patches - 1)], point_sem.at[1])
+    for j in range(1, slabs):
+        point_second(j).start()
     with jax.named_scope("place"):
-        sides = [jnp.where(from_p[m], side_in[m].astype(F32), 0.0) for m in range(2)]
-        tips = [
-            jnp.where(jnp.logical_and(from_s[n], from_p[m]), tip_in[2 * n + m].astype(F32), 0.0) for n, m in corners
-        ]
-        stack = join(*sides, *tips).astype(BF16)
-        placed_v = dot(dot_nt(words, stack).astype(BF16), place_v)
-        placed_r = dot(dot_nt(rest, stack).astype(BF16), place_r)
-
-        def piece(x, r):
-            return x[:, (r + ex) * wide_lanes : (r + ex + 1) * wide_lanes]
+        stack = rim[...]
+        placed_v = dot_nt(words, stack)
+        placed_r = dot_nt(rest, stack)
+
+        def rim_row(base, at, ok):
+            return jnp.where(ok, rim[base + at : base + at + 1, :wide_lanes].astype(F32), 0.0)
 
         def framed(middle, before, after):
             before, after = pltpu.roll(before, ey, 1), pltpu.roll(after, ey, 1)
             return jnp.where(low_half, middle, jnp.where(tail_half, after, before))
 
-        w_at = ex * (2 * SWEEPS - 1)
         w_rows = {}
         for i in range(ex):
-            ends = [sides[m][w_at + i : w_at + i + 1, :wide_lanes] for m in range(2)]
-            w_rows[i] = framed(w_own[i : i + 1], *ends)
-        w_tips = [[tips[2 * n + m][4:5, :wide_lanes] for m in range(2)] for n in range(2)]
+            w_rows[i] = framed(
+                w_own[i : i + 1],
+                rim_row(side_base[0], i, has_prev_p),
+                rim_row(side_base[1], side_w + i, has_next_p),
+            )
+        w_tips = [
+            (
+                rim_row(tip_base[n][0], 5, jnp.logical_and(from_s[n], has_prev_p)),
+                rim_row(tip_base[n][1], 0, jnp.logical_and(from_s[n], has_next_p)),
+            )
+            for n in range(2)
+        ]
+        edges_v, edges_r = {}, {}
+        for i in range(ex):
+            edges_v[i] = framing(placed_v, SWEEPS * i, masks[None, SWEEPS])
+            edges_r[i] = framing(placed_r, SWEEPS * ex + (SWEEPS - 1) * i, masks[None, SWEEPS - 1])
+        for n in range(2):
+            r1, r2 = (-1, -2) if n == 0 else (ex, ex + 1)
+            base = tip_base[n][1]
+            used = join(placed_v[:DEEP], placed_v[2 * DEEP : 5 * DEEP])
+            edges_v[r1] = framing(used, base + 2, masks[n, 2])
+            edges_v[r2] = framing(used, base + 4, masks[n, 1])
+            edges_r[r1] = framing(placed_r[:DEEP], base + 5, masks[n, 1])
 
     with jax.named_scope("w_near"):
         for n in range(2):
@@ -435,8 +478,8 @@
 
     with jax.named_scope("stencil"):
         by_d, by_x, by_y, by_r2, by_r1, by_r0 = {}, {}, {}, {}, {}, {}
-        for i, (v_half, r_half) in enumerate(zip(halves(own_v), halves(own_r))):
-            full, side = v_half + piece(placed_v, i), r_half + piece(placed_r, i)
+        for i, (v_half, r_half) in enumerate(own_rows):
+            full, side = v_half + edges_v[i], r_half + edges_r[i]
             by_d[i], by_x[i], by_y[i] = (full[k * 2 * DEEP : (k + 1) * 2 * DEEP] for k in range(3))
             by_r2[i], by_r1[i], by_r0[i] = (
                 side[: 2 * DEEP], side[2 * DEEP : 2 * DEEP + 3 * comps], side[3 * DEEP : 3 * DEEP + comps]
@@ -445,11 +488,13 @@
             got = jnp.where(from_s[n], near_in[n].astype(F32), 0.0)
             for i, half in enumerate(halves(got)):
                 r = i - ex if n == 0 else i + ex
-                edge_v, edge_r = piece(placed_v, r), piece(placed_r, r)
-                by_d[r] = half[0:DEEP] + edge_v[0:DEEP]
-                by_x[r] = half[DEEP : 3 * DEEP] + edge_v[2 * DEEP : 4 * DEEP]
-                by_y[r] = half[3 * DEEP : 4 * DEEP] + edge_v[4 * DEEP : 5 * DEEP]
-                by_r2[r] = half[4 * DEEP : 5 * DEEP] + edge_r[0:DEEP]
+                edge = edges_v[r]
+                by_d[r] = half[0:DEEP] + edge[0:DEEP]
+                by_x[r] = half[DEEP : 3 * DEEP] + edge[DEEP : 3 * DEEP]
+                by_y[r] = half[3 * DEEP : 4 * DEEP] + edge[3 * DEEP : 4 * DEEP]
+                by_r2[r] = half[4 * DEEP : 5 * DEEP]
+                if r in edges_r:
+                    by_r2[r] = by_r2[r] + edges_r[r]
                 by_r1[r] = half[3 * DEEP - comps - 1 : 3 * DEEP - 1]
                 w_rows[r] = half[3 * DEEP - 1 : 3 * DEEP]
                 if r in (-1, ex):
@@ -482,18 +527,9 @@
                 two[r][comps : 2 * comps]
                 + w_rows[r] * (x_part + turn(two[r][2 * comps : 3 * comps]) + by_r0[r])
             )
-        traction = jnp.where(low_half, drawn[0], pltpu.roll(drawn[1], ey, 1)).astype(BF16)
+        tractions = [jnp.where(low_half, x, 0.0).astype(BF16) for x in drawn]
         for owner in range(patches):
-            pull_out[owner] = dot(traction, onehot_elem[owner]).astype(BF16)
-    for n in range(1, len(reaches)):
-        with jax.named_scope("w_reach"):
-            near_wait(n)
-        if n + 1 < len(reaches):
-            near_signal(n + 1)
-    with jax.named_scope("w_pt1"):
-        settle(points.at[s, pl.ds(0, patches - 1)], point_sem.at[1])
-    for j in range(1, slabs):
-        point_second(j).start()
+            pull_out[owner] = sum(dot(tractions[i], onehot_elem[owner, i]) for i in range(ex)).astype(BF16)
     with jax.named_scope("s_pull"):
         for j in sorted(range(slabs), key=lambda j: -min(j, slabs - j)):
             for i in range(patches):
@@ -510,15 +546,21 @@
         rounded = vb[k]
         wide = rounded.astype(F32)
         with jax.named_scope("w_halo"):
-            pl.when(has_prev_p)(lambda: y_up(k).wait_recv())
-            pl.when(has_next_p)(lambda: y_down(k).wait_recv())
+            if k > 0:
+                pl.when(has_prev_p)(lambda: y_up(k).wait_recv())
+                pl.when(has_next_p)(lambda: y_down(k).wait_recv())
             pl.when(has_prev_s)(lambda: x_up(k).wait_recv())
             pl.when(has_next_s)(lambda: x_down(k).wait_recv())
         line = lax.broadcasted_iota(jnp.int32, (ey, dof), 0)
         along_y = []
         for i in range(ex):
-            before = halo_y[k, 0, i].astype(F32)[PACK - 1 : PACK]
-            after = halo_y[k, 1, i].astype(F32)[0:1]
+            if k == 0:
+                at = shift + side_v + SWEEPS * (i + 1) - 1
+                before = rim[at : at + 1].astype(F32)
+                after = rim[SWEEPS * i : SWEEPS * i + 1].astype(F32)
+            else:
+                before = halo_y[k, 0, i].astype(F32)[PACK - 1 : PACK]
+                after = halo_y[k, 1, i].astype(F32)[0:1]
             before = jnp.where(has_prev_p, before, 0.0)
             after = jnp.where(has_next_p, after, 0.0)
             prev = jnp.where(line == 0, jnp.broadcast_to(before, (ey, dof)), pltpu.roll(wide[i], 1, 0))
@@ -584,11 +626,11 @@
     acc = scatter(s, jnp.zeros((comps * rows, cols), F32))
     with jax.named_scope("gather1"):
         acc = lax.fori_loop(1, half, gathered, acc)
-    with jax.named_scope("build2"):
-        lax.fori_loop(half, slabs, prepared, 0)
     with jax.named_scope("sweep1"):
         keep(sweep(1, fluid_ref), 2)
         send_halos(2)
+    with jax.named_scope("build2"):
+        lax.fori_loop(half, slabs, prepared, 0)
     with jax.named_scope("gather2"):
         acc = lax.fori_loop(half, slabs, gathered, acc)
     loads = acc.reshape(comps, rows, cols)
@@ -599,7 +641,7 @@
         spread = dot(narrow, onehot_col[s, :, span]).reshape(comps, rows, cap)
         hot = onehot_row[s, :, span].astype(F32)
         for c in range(comps):
-            picks_out[k, c : c + 1] = jnp.sum(spread[c] * hot, axis=0, keepdims=True)
+            picks_out[k, c : c + 1] = jnp.sum(spread[c] * hot, axis=0, keepdims=True).astype(BF16)
     with jax.named_scope("s_pick"):
         for j in range(1, patches):
             pick_copy(j).start()
@@ -614,16 +656,14 @@
     for k in range(patches):
         live = lives(k)
         for c in range(comps):
-            wall_ref[c, 0, :, k * cap : (k + 1) * cap] = jnp.where(live, picks_in[k, c : c + 1], 0.0)
+            wall_ref[c, 0, :, k * cap : (k + 1) * cap] = jnp.where(live, picks_in[k, c : c + 1].astype(F32), 0.0)
 
     with jax.named_scope("drain"):
         halo_sends(SWEEPS - 1, lambda copy: copy.wait_send())
         pl.when(has_next_p)(lambda: d_up().wait_send())
         pl.when(has_prev_p)(lambda: d_down().wait_send())
         for n in range(2):
-            pl.when(to_s[n])(lambda: near_copy(n).wait_send())
             pl.when(to_far[n])(lambda: far_copy(n).wait_send())
-            pl.when(to_p[n])(lambda: side_copy(n).wait_send())
         for n, m in corners:
             pl.when(jnp.logical_and(to_s[n], to_p[m]))(lambda: tip_copy(n, m).wait_send())
         settle(points.at[s, pl.ds(0, patches - 1)], point_sem.at[0])
@@ -672,9 +712,9 @@
             pltpu.VMEM((slabs, patches, 1, cap), jnp.int32),
             pltpu.VMEM((slabs, comps, patches * cap), BF16),
             pltpu.VMEM((patches, comps, cap), BF16),
-            pltpu.VMEM((patches, comps, cap), F32),
-            pltpu.VMEM((patches, comps, cap), F32),
-            pltpu.VMEM((patches, ex * ey, cap), BF16),
+            pltpu.VMEM((patches, comps, cap), BF16),
+            pltpu.VMEM((patches, comps, cap), BF16),
+            pltpu.VMEM((patches, ex, ex * ey, cap), BF16),
             pltpu.VMEM((slabs, rows, patches * cap), BF16),
             pltpu.VMEM((slabs, cols, patches * cap), BF16),
             pltpu.VMEM((comps, rows, cols), F32),
@@ -685,13 +725,10 @@
             pltpu.VMEM((8, ex * ey), BF16),
             pltpu.VMEM((2, 8, ex * ey), BF16),
             pltpu.VMEM((2, DEEP, dof), BF16),
-            pltpu.VMEM((2, DEEP, dof), BF16),
             pltpu.VMEM((4, TIP, dof), BF16),
-            pltpu.VMEM((4, TIP, dof), BF16),
+            pltpu.VMEM((ex * ey, dof), BF16),
             sem((8,)),
-            sem((2,)),
             sem((2, 2)),
-            sem((2,)),
             sem((2, 2)),
             sem((2,)),
             sem((2,)),

time: 21.1 us -> 20.2 us (0.957)
  Pallas kernels: 20.3 us -> 19.4 us
    pallas_call x1, Pallas kernels: 19.6 us -> 18.7 us  [shards(): pl.pallas_call(functools.partial(kernel, slabs, patches, len(args)), out_...]
where the time goes in v4:
time: 20.2 us; the launch traced here: 20.1 us
  Pallas kernels  19.4 us (96%)
  between operations  0.64 us (3%)
    pallas_call x1, Pallas kernels, shards(): pl.pallas_call(functools.partial(kernel, slabs, patches, len(args)), out_...  18.7 us
    pallas_call x1, Pallas kernels, shards(): pl.pallas_call(deliver, out_shape=tuple((jax.ShapeDtypeStruct(x.shape, x....  0.71 us

profile of v4, /device:TPU:0, one launch (start us, length us, event | category | flops | bytes accessed | tf_op | source)
XLA Modules:
  0.0 20.1 jit_solution(8821288497051143480)
XLA Ops:
  0.6 18.7 %shard_map.148 = (f32[2,64,256]{2,1,0:T(8,128)S(1)}, f32[3,64,128]{2,1,0:T(8,128)S(1)}, f32[3,1,1,1024]{3,2,1,0:T(1,128)S(1)}) custom-call(f32[2,64,256]{2,1,0:T(8,128)} %refs_0_.1, f32[2,64,256]{2,1,0:T(8,128)} %refs_1_.1, f32[2,64]{1,0:T(2,128)} %refs_2_.1, bf16[256,256]{1,0:T(8,128)(2,1)} %refs_3_.1, bf16[256,256]{1,0:T(8,128)(2,1)} %refs_4_.1, ...), custom_call_target="tpu_custom_call" | custom-call | tf_op jit(solution)/shard_map/pallas_call | solution.py:692
  19.4 0.7 %shard_map.149 = (f32[2,64,256]{2,1,0:T(8,128)}, f32[3,64,128]{2,1,0:T(8,128)}, f32[3,1,1,1024]{3,2,1,0:T(1,128)}) custom-call(f32[2,64,256]{2,1,0:T(8,128)S(1)} %get-tuple-element.6.refs_0_, f32[3,64,128]{2,1,0:T(8,128)S(1)} %get-tuple-element.7.refs_1_, f32[3,1,1,1024]{3,2,1,0:T(1,128)S(1)} %get-tuple-element.8.refs_2_), custom_call_target="tpu_custom_call" | custom-call | tf_op jit(solution)/shard_map/pallas_call | solution.py:752

commit v5 on v4

--- a/solution.py
+++ b/solution.py
@@ -13,7 +13,7 @@
 SPARE = 8 * 2**20
 DEEP = 16
 TIP = 8
-LOAD_ORDER = (7, 6, 3, 4, 5, 2, 0, 1, 9, 8, 10, 11, 12)
+LOAD_ORDER = (7, 6, 3, 4, 5, 0, 1, 2, 9, 8, 10, 11, 12)
 MESH = pl.DeviceIdType.MESH
 F32 = jnp.float32
 BF16 = jnp.bfloat16
@@ -57,50 +57,57 @@
     return jnp.zeros((rows, cols), F32)
 
 
-def make_words(traction, inverse, matrix, couple_x, couple_y):
-    comps, dof = traction.shape
-    base0 = dot_nt(traction, inverse)
+def first_words(base0, traction, matrix, couple_x, couple_y):
     low = base0.astype(BF16)
-    one = join(dot_nt(low, couple_x), traction.astype(F32) - dot_nt(low, matrix), dot_nt(low, couple_y))
-    base1 = dot_nt(one.astype(BF16), inverse)
+    return join(dot_nt(low, couple_x), traction.astype(F32) - dot_nt(low, matrix), dot_nt(low, couple_y))
+
+
+def second_words(base1, one, comps, matrix, couple_x, couple_y):
     low = base1.astype(BF16)
     by_x, by_y = dot_nt(low, couple_x), dot_nt(low, couple_y)
     by_d = one - dot_nt(low, matrix)
-    two = join(
+    dof = one.shape[1]
+    return join(
         by_d[:comps], by_x, by_y[:comps], blank(DEEP - 5 * comps, dof),
         by_d[comps:], by_y[comps:], blank(DEEP - 4 * comps, dof),
     )
-    base2 = dot_nt(two.astype(BF16), inverse)
+
+
+def third_words(base2, two, matrix, couple_x, couple_y):
     low = base2.astype(BF16)
-    three = join(two - dot_nt(low, matrix), dot_nt(low, couple_x), dot_nt(low, couple_y))
-    rest = join(base2, base1, blank(DEEP - 3 * comps, dof), base0, blank(DEEP - comps, dof))
-    return three.astype(BF16), rest.astype(BF16)
+    return join(two - dot_nt(low, matrix), dot_nt(low, couple_x), dot_nt(low, couple_y)).astype(BF16)
+
+
+def stacked(two, one, none):
+    comps, dof = none.shape
+    return join(two, one, blank(DEEP - 3 * comps, dof), none, blank(DEEP - comps, dof)).astype(BF16)
 
 
 def kernel(slabs, patches, args, *refs):
     hbm, refs = refs[:args], refs[args:]
     (fluid_ref, net_ref, wall_ref), refs = refs[:3], refs[3:]
-    (state_ref, rhs_ref, scale_ref, matrices, traction_ref, slots, count_ref, nets) = refs[:8]
-    refs = refs[8:]
-    cx_ref, cy_ref, inverse_ref, matrix_ref = (matrices.at[n] for n in range(4))
+    (state_ref, rhs_ref, scale_ref, matrices, traction_ref, slots, count_ref, nets, inverse_ref) = refs[:9]
+    refs = refs[9:]
+    cx_ref, cy_ref, matrix_ref = (matrices.at[n] for n in range(3))
     elem_ref, point_ref = slots.at[0], slots.at[1]
     (vb, halo_x, halo_y, halo_d, points, pulls, pull_out, picks_out, picks_in) = refs[:9]
     (onehot_elem, onehot_row, onehot_col, rest_buf, gain_buf, base_buf) = refs[9:15]
     (near_out, near_in, far_out, far_in, side_out, tip_out, rim) = refs[15:22]
-    (load_sem, rx, ry, sd, rd, point_sem, rp2, pull_sem, rq, pick_sem) = refs[22:32]
-    (s_near, r_near, s_far, r_far, s_side, r_side, s_tip, r_tip, near_sem) = refs[32:]
-    sx, sy = s_near, s_side
+    (load_sem, rx, ry, rd, point_sem, rp2, pull_sem, rq, pick_sem) = refs[22:31]
+    (r_near, s_far, r_far, r_side, r_tip, near_sem) = refs[31:]
+    s_near, s_side, s_tip = load_sem.at[pl.ds(0, 2)], load_sem.at[pl.ds(2, 2)], load_sem.at[pl.ds(4, 4)]
+    sx, sy, sd = s_near, s_side, s_far
     comps = nets.shape[0] - 1
     disp_ref, stiff_ref = nets.at[pl.ds(0, comps)], nets.at[comps]
     homes = (
-        (state_ref, 0), (rhs_ref, 1), (scale_ref, 2), (matrix_ref, 3), (cx_ref, 3), (cy_ref, 3), (inverse_ref, 3),
+        (state_ref, 0), (rhs_ref, 1), (scale_ref, 2), (matrix_ref, 3), (cx_ref, 3), (cy_ref, 3), (inverse_ref, 8),
         (traction_ref, 4), (elem_ref, 5), (point_ref, 5), (count_ref, 6), (disp_ref, 7), (stiff_ref, 7),
     )
 
     loads_in = [pltpu.make_async_copy(hbm[n], homes[n][0], load_sem.at[homes[n][1]]) for n in range(args)]
     for n in LOAD_ORDER:
         loads_in[n].start()
-    groups = (state_ref, rhs_ref, scale_ref, matrices, traction_ref, slots, count_ref, nets)
+    groups = (state_ref, rhs_ref, scale_ref, matrices, traction_ref, slots, count_ref, nets, inverse_ref)
 
     def ready(*names):
         for n in names:
@@ -288,26 +295,30 @@
             rest_buf[c] = disp_ref[c] - stiff_ref[...] * full * gain
 
     with jax.named_scope("w_mat"):
-        ready(4, 3)
-    with jax.named_scope("words"):
-        words, rest = make_words(
-            traction_ref[...], inverse_ref[...], matrix_ref[...], cx_ref[...], cy_ref[...]
-        )
-    ready(2)
+        ready(4, 8)
+        base0 = dot_nt(traction_ref[...], inverse_ref[...])
+        ready(3, 0, 1, 2)
+    rounded0 = state_ref[...].astype(BF16)
+    vb[0] = rounded0
+    wet = rhs_ref[...].astype(BF16)
     flat = 1.0 / scale_ref[...]
     w_own = jnp.concatenate([flat, blank(ex, wide_lanes - ey)], axis=1)
-    ready(0)
-    rounded0 = state_ref[...].astype(BF16)
-    vb[0] = rounded0
-    ready(1)
-    wet = rhs_ref[...].astype(BF16)
     lane = lax.broadcasted_iota(jnp.int32, (1, wide_lanes), 1)
     low_half = lane < ey
     tail_half = lane < ey + ey // 2
     w_lines = jnp.concatenate([w_own] + [blank(ex, wide_lanes)] * (dof // wide_lanes - 1), axis=1)
     with jax.named_scope("project"):
-        own_v = dot_nt(words, rounded0.reshape(wide_lanes, dof))
-        own_r = dot_nt(rest, wet.reshape(wide_lanes, dof))
+        couples = (matrix_ref[...], cx_ref[...], cy_ref[...])
+        one = first_words(base0, traction_ref[...], *couples)
+        base1 = dot_nt(one.astype(BF16), inverse_ref[...])
+        two = second_words(base1, one, comps, *couples)
+        flow = rounded0.reshape(wide_lanes, dof)
+        passed = join(*[dot(flow, couple) for couple in couples]).astype(BF16)
+        mapped = dot(join(passed, wet.reshape(wide_lanes, dof)), inverse_ref[...])
+        turned = join(flow.astype(F32) - mapped[:wide_lanes], mapped[wide_lanes:]).astype(BF16)
+        both = dot_nt(stacked(two, one, traction_ref[...].astype(F32)), turned)
+        own_v = join(*[both[: 2 * DEEP, n * wide_lanes : (n + 1) * wide_lanes] for n in range(3)])
+        own_r = both[:, 3 * wide_lanes :]
         packed = jnp.where(low_half, w_own[0:1], pltpu.roll(w_own[1:2], ey, 1))
         spare = join(
             blank(2 * DEEP - comps - 1, wide_lanes), own_r[2 * DEEP : 2 * DEEP + comps], packed
@@ -346,6 +357,7 @@
                     tip = [*near2[::-1], blank(1, dof), *last, weigh, blank(TIP - 6, dof)]
                 tip_out[2 * n + m] = join(*tip).astype(BF16)
 
+    ready(5, 6, 7)
     with jax.named_scope("w_barrier"):
         pl.semaphore_wait(barrier, awaited)
     for n, m in corners:
@@ -358,13 +370,8 @@
         pl.when(to_far[n])(lambda: far_copy(n).start())
     if reaches:
         near_signal(0)
-    ready(5)
     for j in range(1, patches):
         point_first(j).start()
-    ready(7)
-    pl.when(has_next_p)(lambda: d_up().start())
-    pl.when(has_prev_p)(lambda: d_down().start())
-    ready(6)
     for owner in range(patches):
 
         @pl.when(p == owner)
@@ -391,8 +398,14 @@
         for i in range(ex):
             base_buf[i] = rhs_ref[i] - scales[i] * own[i]
 
-    with jax.named_scope("shell"):
-        shell()
+    for n in range(2):
+        pl.when(to_far[n])(lambda: far_copy(n).wait_send())
+    pl.when(has_next_p)(lambda: d_up().start())
+    pl.when(has_prev_p)(lambda: d_down().start())
+    with jax.named_scope("late_words"):
+        base2 = dot_nt(two.astype(BF16), inverse_ref[...])
+        words = third_words(base2, two, matrix_ref[...], cx_ref[...], cy_ref[...])
+        rest = stacked(base2, base1, base0)
     with jax.named_scope("prelude"):
         prelude(0)
 
@@ -619,6 +632,8 @@
 
     half = (slabs + 1) // 2
     build_points(s)
+    with jax.named_scope("shell"):
+        shell()
     with jax.named_scope("build1"):
         lax.fori_loop(1, half, prepared, 0)
     with jax.named_scope("w_own"):
@@ -662,8 +677,6 @@
         halo_sends(SWEEPS - 1, lambda copy: copy.wait_send())
         pl.when(has_next_p)(lambda: d_up().wait_send())
         pl.when(has_prev_p)(lambda: d_down().wait_send())
-        for n in range(2):
-            pl.when(to_far[n])(lambda: far_copy(n).wait_send())
         for n, m in corners:
             pl.when(jnp.logical_and(to_s[n], to_p[m]))(lambda: tip_copy(n, m).wait_send())
         settle(points.at[s, pl.ds(0, patches - 1)], point_sem.at[0])
@@ -700,11 +713,12 @@
         out_specs=(vmem, vmem, vmem),
         scratch_shapes=[pltpu.VMEM(x.shape, x.dtype) for x in args[:3]]
         + [
-            pltpu.VMEM((4,) + args[3].shape, BF16),
+            pltpu.VMEM((3,) + args[3].shape, BF16),
             pltpu.VMEM(args[7].shape, BF16),
             pltpu.VMEM((2,) + elem.shape, jnp.int32),
             pltpu.VMEM(args[10].shape, jnp.int32),
             pltpu.VMEM((comps + 1, rows, cols), F32),
+            pltpu.VMEM(args[6].shape, BF16),
             pltpu.VMEM((SWEEPS, ex, ey, dof), BF16),
             pltpu.VMEM((SWEEPS, 2, ey, dof), BF16),
             pltpu.VMEM((SWEEPS, 2, ex, PACK, dof), BF16),
@@ -727,10 +741,9 @@
             pltpu.VMEM((2, DEEP, dof), BF16),
             pltpu.VMEM((4, TIP, dof), BF16),
             pltpu.VMEM((ex * ey, dof), BF16),
-            sem((8,)),
+            sem((9,)),
             sem((2, 2)),
             sem((2, 2)),
-            sem((2,)),
             sem((2,)),
             sem((3,)),
             sem((slabs,)),
@@ -741,9 +754,6 @@
             sem((2,)),
             sem((2,)),
             sem((2,)),
-            sem((2,)),
-            sem((2,)),
-            sem((4,)),
             sem((4,)),
             pltpu.SemaphoreType.REGULAR((max(slabs.bit_length() - 2, 1),)),
         ],

time: 20.2 us -> 19.9 us (0.985)
  Pallas kernels: 19.4 us -> 19.1 us
    pallas_call x1, Pallas kernels: 18.7 us -> 18.4 us  [shards(): pl.pallas_call(functools.partial(kernel, slabs, patches, len(args)), out_...]
where the time goes in v5:
time: 19.9 us; the launch traced here: 19.8 us
  Pallas kernels  19.1 us (96%)
  between operations  0.64 us (3%)
    pallas_call x1, Pallas kernels, shards(): pl.pallas_call(functools.partial(kernel, slabs, patches, len(args)), out_...  18.4 us
    pallas_call x1, Pallas kernels, shards(): pl.pallas_call(deliver, out_shape=tuple((jax.ShapeDtypeStruct(x.shape, x....  0.71 us

profile of v5, /device:TPU:0, one launch (start us, length us, event | category | flops | bytes accessed | tf_op | source)
XLA Modules:
  0.0 19.8 jit_solution(12199846354178593974)
XLA Ops:
  0.6 18.4 %shard_map.148 = (f32[2,64,256]{2,1,0:T(8,128)S(1)}, f32[3,64,128]{2,1,0:T(8,128)S(1)}, f32[3,1,1,1024]{3,2,1,0:T(1,128)S(1)}) custom-call(f32[2,64,256]{2,1,0:T(8,128)} %refs_0_.1, f32[2,64,256]{2,1,0:T(8,128)} %refs_1_.1, f32[2,64]{1,0:T(2,128)} %refs_2_.1, bf16[256,256]{1,0:T(8,128)(2,1)} %refs_3_.1, bf16[256,256]{1,0:T(8,128)(2,1)} %refs_4_.1, ...), custom_call_target="tpu_custom_call" | custom-call | tf_op jit(solution)/shard_map/pallas_call | solution.py:705
  19.1 0.7 %shard_map.149 = (f32[2,64,256]{2,1,0:T(8,128)}, f32[3,64,128]{2,1,0:T(8,128)}, f32[3,1,1,1024]{3,2,1,0:T(1,128)}) custom-call(f32[2,64,256]{2,1,0:T(8,128)S(1)} %get-tuple-element.6.refs_0_, f32[3,64,128]{2,1,0:T(8,128)S(1)} %get-tuple-element.7.refs_1_, f32[3,1,1,1024]{3,2,1,0:T(1,128)S(1)} %get-tuple-element.8.refs_2_), custom_call_target="tpu_custom_call" | custom-call | tf_op jit(solution)/shard_map/pallas_call | solution.py:762

commit v6 on v5

--- a/solution.py
+++ b/solution.py
@@ -297,7 +297,13 @@
     with jax.named_scope("w_mat"):
         ready(4, 8)
         base0 = dot_nt(traction_ref[...], inverse_ref[...])
-        ready(3, 0, 1, 2)
+        ready(3)
+    couples = (matrix_ref[...], cx_ref[...], cy_ref[...])
+    with jax.named_scope("words"):
+        one = first_words(base0, traction_ref[...], *couples)
+        base1 = dot_nt(one.astype(BF16), inverse_ref[...])
+    with jax.named_scope("w_state"):
+        ready(0, 1, 2)
     rounded0 = state_ref[...].astype(BF16)
     vb[0] = rounded0
     wet = rhs_ref[...].astype(BF16)
@@ -308,9 +314,6 @@
     tail_half = lane < ey + ey // 2
     w_lines = jnp.concatenate([w_own] + [blank(ex, wide_lanes)] * (dof // wide_lanes - 1), axis=1)
     with jax.named_scope("project"):
-        couples = (matrix_ref[...], cx_ref[...], cy_ref[...])
-        one = first_words(base0, traction_ref[...], *couples)
-        base1 = dot_nt(one.astype(BF16), inverse_ref[...])
         two = second_words(base1, one, comps, *couples)
         flow = rounded0.reshape(wide_lanes, dof)
         passed = join(*[dot(flow, couple) for couple in couples]).astype(BF16)
@@ -437,15 +440,34 @@
             pl.when(from_p[m])(lambda: side_copy(m).wait_recv())
         for n, m in corners:
             pl.when(jnp.logical_and(from_s[n], from_p[m]))(lambda: tip_copy(n, m).wait_recv())
-    for n in range(1, len(reaches)):
-        with jax.named_scope("w_reach"):
-            near_wait(n)
-        if n + 1 < len(reaches):
-            near_signal(n + 1)
+    early = s < slabs // 2
+    known = 4
+
+    def far_off(j):
+        peer = slab_peer(j)
+        return jnp.maximum(peer - s, s - peer) > known
+
+    def learn_all():
+        for n in range(1, len(reaches)):
+            with jax.named_scope("w_reach"):
+                near_wait(n)
+            if n + 1 < len(reaches):
+                near_signal(n + 1)
+
     with jax.named_scope("w_pt1"):
         settle(points.at[s, pl.ds(0, patches - 1)], point_sem.at[1])
-    for j in range(1, slabs):
-        point_second(j).start()
+
+    @pl.when(early)
+    def _():
+        for j in range(1, slabs):
+            pl.when(jnp.logical_not(far_off(j)))(lambda: point_second(j).start())
+
+    @pl.when(jnp.logical_not(early))
+    def _():
+        learn_all()
+        for j in range(1, slabs):
+            point_second(j).start()
+
     with jax.named_scope("place"):
         stack = rim[...]
         placed_v = dot_nt(words, stack)
@@ -543,11 +565,26 @@
         tractions = [jnp.where(low_half, x, 0.0).astype(BF16) for x in drawn]
         for owner in range(patches):
             pull_out[owner] = sum(dot(tractions[i], onehot_elem[owner, i]) for i in range(ex)).astype(BF16)
+    order = sorted(range(slabs), key=lambda j: -min(j, slabs - j))
+
+    def send_pulls(j):
+        for i in range(patches):
+            if (j, i) != (0, 0):
+                pull_copy(j, i).start()
+
     with jax.named_scope("s_pull"):
-        for j in sorted(range(slabs), key=lambda j: -min(j, slabs - j)):
-            for i in range(patches):
-                if (j, i) != (0, 0):
-                    pull_copy(j, i).start()
+
+        @pl.when(early)
+        def _():
+            for j in order:
+                pl.when(jnp.logical_not(far_off(j)))(lambda: send_pulls(j))
+        @pl.when(jnp.logical_not(early))
+        def _():
+            for j in range(1, slabs):
+                pl.when(far_off(j))(lambda: send_pulls(j))
+            for j in order:
+                pl.when(jnp.logical_not(far_off(j)))(lambda: send_pulls(j))
+
     for owner in range(patches):
 
         @pl.when(p == owner)
@@ -604,6 +641,17 @@
         send_halos(1)
         prelude(1)
 
+    @pl.when(early)
+    def _():
+        learn_all()
+        for j in order[:-1]:
+
+            @pl.when(far_off(j))
+            def _():
+                point_second(j).start()
+                send_pulls(j)
+
+
     def scatter(slab, acc):
         hot = onehot_row[slab]
         value = pulls[slab]
@@ -617,18 +665,29 @@
         alternate = jnp.where(lax.rem(t, 2) == 1, s + step, s - step)
         return jnp.where(t <= 2 * inner, alternate, jnp.where(s < slabs - 1 - s, t, slabs - 1 - t))
 
+    def settle_points(t):
+        with jax.named_scope("w_point"):
+            settle(points.at[nearest(t)], rp2.at[nearest(t)])
+
+    def settle_pulls(t):
+        with jax.named_scope("w_pull"):
+            settle(pulls.at[nearest(t)], rq.at[nearest(t)])
+
     def prepared(t, carry):
-        slab = nearest(t)
-        with jax.named_scope("w_point"):
-            settle(points.at[slab], rp2.at[slab])
-        build_points(slab)
+        settle_points(t)
+        build_points(nearest(t))
         return carry
 
     def gathered(t, acc):
-        slab = nearest(t)
-        with jax.named_scope("w_pull"):
-            settle(pulls.at[slab], rq.at[slab])
-        return scatter(slab, acc)
+        settle_pulls(t)
+        return scatter(nearest(t), acc)
+
+    def gathered_ahead(t, acc):
+        settle_points(t + half - 1)
+        settle_pulls(t)
+        acc = scatter(nearest(t), acc)
+        build_points(nearest(t + half - 1))
+        return acc
 
     half = (slabs + 1) // 2
     build_points(s)
@@ -639,27 +698,32 @@
     with jax.named_scope("w_own"):
         settle(pulls.at[s, :, pl.ds(0, (patches - 1) * cap)], rq.at[s])
     acc = scatter(s, jnp.zeros((comps * rows, cols), F32))
+    last = slabs - half + 1
     with jax.named_scope("gather1"):
-        acc = lax.fori_loop(1, half, gathered, acc)
+        acc = lax.fori_loop(1, half, gathered_ahead, acc)
     with jax.named_scope("sweep1"):
         keep(sweep(1, fluid_ref), 2)
         send_halos(2)
-    with jax.named_scope("build2"):
-        lax.fori_loop(half, slabs, prepared, 0)
     with jax.named_scope("gather2"):
-        acc = lax.fori_loop(half, slabs, gathered, acc)
+        acc = lax.fori_loop(half, last, gathered_ahead, acc)
+        acc = lax.fori_loop(last, slabs, gathered, acc)
     loads = acc.reshape(comps, rows, cols)
     fresh = [rest_buf[c] + loads[c] * gain_buf[...] for c in range(comps)]
     narrow = jnp.concatenate([x.astype(BF16) for x in fresh], axis=0)
-    for k in range(patches):
-        span = pl.ds(k * cap, cap)
+    def picks_for(j):
+        k = patch_peer(j)
+        span = pl.ds(pl.multiple_of(k * cap, cap), cap)
         spread = dot(narrow, onehot_col[s, :, span]).reshape(comps, rows, cap)
         hot = onehot_row[s, :, span].astype(F32)
         for c in range(comps):
             picks_out[k, c : c + 1] = jnp.sum(spread[c] * hot, axis=0, keepdims=True).astype(BF16)
+
+    far_first = sorted(range(1, patches), key=lambda j: -min(j, patches - j))
     with jax.named_scope("s_pick"):
-        for j in range(1, patches):
+        for j in far_first:
+            picks_for(j)
             pick_copy(j).start()
+    picks_for(0)
     picks_in[p] = picks_out[p]
     for c in range(comps):
         net_ref[c] = fresh[c]

time: 19.9 us -> 19.7 us (0.990)
  Pallas kernels: 19.1 us -> 18.9 us
    pallas_call x1, Pallas kernels: 18.4 us -> 18.2 us  [shards(): pl.pallas_call(functools.partial(kernel, slabs, patches, len(args)), out_...]
where the time goes in v6:
time: 19.7 us; the launch traced here: 19.5 us
  Pallas kernels  18.9 us (96%)
  between operations  0.64 us (3%)
    pallas_call x1, Pallas kernels, shards(): pl.pallas_call(functools.partial(kernel, slabs, patches, len(args)), out_...  18.2 us
    pallas_call x1, Pallas kernels, shards(): pl.pallas_call(deliver, out_shape=tuple((jax.ShapeDtypeStruct(x.shape, x....  0.71 us

profile of v6, /device:TPU:0, one launch (start us, length us, event | category | flops | bytes accessed | tf_op | source)
XLA Modules:
  0.0 19.5 jit_solution(222803573445815293)
XLA Ops:
  0.6 18.2 %shard_map.148 = (f32[2,64,256]{2,1,0:T(8,128)S(1)}, f32[3,64,128]{2,1,0:T(8,128)S(1)}, f32[3,1,1,1024]{3,2,1,0:T(1,128)S(1)}) custom-call(f32[2,64,256]{2,1,0:T(8,128)} %refs_0_.1, f32[2,64,256]{2,1,0:T(8,128)} %refs_1_.1, f32[2,64]{1,0:T(2,128)} %refs_2_.1, bf16[256,256]{1,0:T(8,128)(2,1)} %refs_3_.1, bf16[256,256]{1,0:T(8,128)(2,1)} %refs_4_.1, ...), custom_call_target="tpu_custom_call" | custom-call | tf_op jit(solution)/shard_map/pallas_call | solution.py:769
  18.8 0.7 %shard_map.149 = (f32[2,64,256]{2,1,0:T(8,128)}, f32[3,64,128]{2,1,0:T(8,128)}, f32[3,1,1,1024]{3,2,1,0:T(1,128)}) custom-call(f32[2,64,256]{2,1,0:T(8,128)S(1)} %get-tuple-element.6.refs_0_, f32[3,64,128]{2,1,0:T(8,128)S(1)} %get-tuple-element.7.refs_1_, f32[3,1,1,1024]{3,2,1,0:T(1,128)S(1)} %get-tuple-element.8.refs_2_), custom_call_target="tpu_custom_call" | custom-call | tf_op jit(solution)/shard_map/pallas_call | solution.py:826

commit v7 on v6

--- a/solution.py
+++ b/solution.py
@@ -506,6 +506,24 @@
             edges_v[r2] = framing(used, base + 4, masks[n, 1])
             edges_r[r1] = framing(placed_r[:DEEP], base + 5, masks[n, 1])
 
+    def across(k, wide):
+        line = lax.broadcasted_iota(jnp.int32, (ey, dof), 0)
+        along_y = []
+        for i in range(ex):
+            if k == 0:
+                at = shift + side_v + SWEEPS * (i + 1) - 1
+                before = rim[at : at + 1].astype(F32)
+                after = rim[SWEEPS * i : SWEEPS * i + 1].astype(F32)
+            else:
+                before = halo_y[k, 0, i].astype(F32)[PACK - 1 : PACK]
+                after = halo_y[k, 1, i].astype(F32)[0:1]
+            before = jnp.where(has_prev_p, before, 0.0)
+            after = jnp.where(has_next_p, after, 0.0)
+            prev = jnp.where(line == 0, jnp.broadcast_to(before, (ey, dof)), pltpu.roll(wide[i], 1, 0))
+            following = jnp.where(line == ey - 1, jnp.broadcast_to(after, (ey, dof)), pltpu.roll(wide[i], ey - 1, 0))
+            along_y.append((prev + following).astype(BF16))
+        return dot(jnp.concatenate(along_y, axis=0), cy_ref[...])
+
     with jax.named_scope("w_near"):
         for n in range(2):
             pl.when(from_far[n])(lambda: far_copy(n).wait_recv())
@@ -565,6 +583,9 @@
         tractions = [jnp.where(low_half, x, 0.0).astype(BF16) for x in drawn]
         for owner in range(patches):
             pull_out[owner] = sum(dot(tractions[i], onehot_elem[owner, i]) for i in range(ex)).astype(BF16)
+        crossed = across(0, vb[0].astype(F32)).reshape(ex, ey, dof)
+        for i in range(ex):
+            base_buf[i] = base_buf[i] + crossed[i]
     order = sorted(range(slabs), key=lambda j: -min(j, slabs - j))
 
     def send_pulls(j):
@@ -601,22 +622,7 @@
                 pl.when(has_next_p)(lambda: y_down(k).wait_recv())
             pl.when(has_prev_s)(lambda: x_up(k).wait_recv())
             pl.when(has_next_s)(lambda: x_down(k).wait_recv())
-        line = lax.broadcasted_iota(jnp.int32, (ey, dof), 0)
-        along_y = []
-        for i in range(ex):
-            if k == 0:
-                at = shift + side_v + SWEEPS * (i + 1) - 1
-                before = rim[at : at + 1].astype(F32)
-                after = rim[SWEEPS * i : SWEEPS * i + 1].astype(F32)
-            else:
-                before = halo_y[k, 0, i].astype(F32)[PACK - 1 : PACK]
-                after = halo_y[k, 1, i].astype(F32)[0:1]
-            before = jnp.where(has_prev_p, before, 0.0)
-            after = jnp.where(has_next_p, after, 0.0)
-            prev = jnp.where(line == 0, jnp.broadcast_to(before, (ey, dof)), pltpu.roll(wide[i], 1, 0))
-            following = jnp.where(line == ey - 1, jnp.broadcast_to(after, (ey, dof)), pltpu.roll(wide[i], ey - 1, 0))
-            along_y.append((prev + following).astype(BF16))
-        side_y = dot(jnp.concatenate(along_y, axis=0), cy_ref[...])
+        side_y = across(k, wide) if k > 0 else 0.0
         low = jnp.where(has_prev_s, halo_x[k, 0].astype(F32), 0.0)
         high = jnp.where(has_next_s, halo_x[k, 1].astype(F32), 0.0)
         along_x = []

time: 19.7 us -> 19.7 us (level)
  no operation moved by 1% of the time
where the time goes in v7:
time: 19.7 us; the launch traced here: 19.5 us
  Pallas kernels  18.9 us (96%)
  between operations  0.64 us (3%)
    pallas_call x1, Pallas kernels, shards(): pl.pallas_call(functools.partial(kernel, slabs, patches, len(args)), out_...  18.1 us
    pallas_call x1, Pallas kernels, shards(): pl.pallas_call(deliver, out_shape=tuple((jax.ShapeDtypeStruct(x.shape, x....  0.71 us

profile of v7, /device:TPU:0, one launch (start us, length us, event | category | flops | bytes accessed | tf_op | source)
XLA Modules:
  0.0 19.5 jit_solution(13151401017463676765)
XLA Ops:
  0.6 18.1 %shard_map.148 = (f32[2,64,256]{2,1,0:T(8,128)S(1)}, f32[3,64,128]{2,1,0:T(8,128)S(1)}, f32[3,1,1,1024]{3,2,1,0:T(1,128)S(1)}) custom-call(f32[2,64,256]{2,1,0:T(8,128)} %refs_0_.1, f32[2,64,256]{2,1,0:T(8,128)} %refs_1_.1, f32[2,64]{1,0:T(2,128)} %refs_2_.1, bf16[256,256]{1,0:T(8,128)(2,1)} %refs_3_.1, bf16[256,256]{1,0:T(8,128)(2,1)} %refs_4_.1, ...), custom_call_target="tpu_custom_call" | custom-call | tf_op jit(solution)/shard_map/pallas_call | solution.py:775
  18.8 0.7 %shard_map.149 = (f32[2,64,256]{2,1,0:T(8,128)}, f32[3,64,128]{2,1,0:T(8,128)}, f32[3,1,1,1024]{3,2,1,0:T(1,128)}) custom-call(f32[2,64,256]{2,1,0:T(8,128)S(1)} %get-tuple-element.6.refs_0_, f32[3,64,128]{2,1,0:T(8,128)S(1)} %get-tuple-element.7.refs_1_, f32[3,1,1,1024]{3,2,1,0:T(1,128)S(1)} %get-tuple-element.8.refs_2_), custom_call_target="tpu_custom_call" | custom-call | tf_op jit(solution)/shard_map/pallas_call | solution.py:832

commit v8 on v7

--- a/solution.py
+++ b/solution.py
@@ -637,14 +637,15 @@
         return [v[i] + update[i] * inverses[i] for i in range(ex)]
 
     def keep(v, k):
+        if k < SWEEPS:
+            for i in range(ex):
+                vb[k, i] = v[i].astype(BF16)
+            send_halos(k)
         for i in range(ex):
             fluid_ref[i] = v[i]
-            if k < SWEEPS:
-                vb[k, i] = v[i].astype(BF16)
 
     with jax.named_scope("sweep0"):
         keep(sweep(0, state_ref), 1)
-        send_halos(1)
         prelude(1)
 
     @pl.when(early)
@@ -709,7 +710,6 @@
         acc = lax.fori_loop(1, half, gathered_ahead, acc)
     with jax.named_scope("sweep1"):
         keep(sweep(1, fluid_ref), 2)
-        send_halos(2)
     with jax.named_scope("gather2"):
         acc = lax.fori_loop(half, last, gathered_ahead, acc)
         acc = lax.fori_loop(last, slabs, gathered, acc)

time: 19.7 us -> 19.7 us (level)
  no operation moved by 1% of the time
where the time goes in v8:
time: 19.7 us; the launch traced here: 19.5 us
  Pallas kernels  18.9 us (96%)
  between operations  0.64 us (3%)
    pallas_call x1, Pallas kernels, shards(): pl.pallas_call(functools.partial(kernel, slabs, patches, len(args)), out_...  18.1 us
    pallas_call x1, Pallas kernels, shards(): pl.pallas_call(deliver, out_shape=tuple((jax.ShapeDtypeStruct(x.shape, x....  0.71 us

profile of v8, /device:TPU:0, one launch (start us, length us, event | category | flops | bytes accessed | tf_op | source)
XLA Modules:
  0.0 19.5 jit_solution(4953663654676677768)
XLA Ops:
  0.6 18.1 %shard_map.148 = (f32[2,64,256]{2,1,0:T(8,128)S(1)}, f32[3,64,128]{2,1,0:T(8,128)S(1)}, f32[3,1,1,1024]{3,2,1,0:T(1,128)S(1)}) custom-call(f32[2,64,256]{2,1,0:T(8,128)} %refs_0_.1, f32[2,64,256]{2,1,0:T(8,128)} %refs_1_.1, f32[2,64]{1,0:T(2,128)} %refs_2_.1, bf16[256,256]{1,0:T(8,128)(2,1)} %refs_3_.1, bf16[256,256]{1,0:T(8,128)(2,1)} %refs_4_.1, ...), custom_call_target="tpu_custom_call" | custom-call | tf_op jit(solution)/shard_map/pallas_call | solution.py:775
  18.8 0.7 %shard_map.149 = (f32[2,64,256]{2,1,0:T(8,128)}, f32[3,64,128]{2,1,0:T(8,128)}, f32[3,1,1,1024]{3,2,1,0:T(1,128)}) custom-call(f32[2,64,256]{2,1,0:T(8,128)S(1)} %get-tuple-element.6.refs_0_, f32[3,64,128]{2,1,0:T(8,128)S(1)} %get-tuple-element.7.refs_1_, f32[3,1,1,1024]{3,2,1,0:T(1,128)S(1)} %get-tuple-element.8.refs_2_), custom_call_target="tpu_custom_call" | custom-call | tf_op jit(solution)/shard_map/pallas_call | solution.py:832
